TPU v7x, 32 devices: a whole 2x2x4 slice. The times are simulated.
32 devices in a mesh: fsdp: 8 (over z, x), tensor: 4 (over y, core).
Axes of the slice: x: 2, y: 2, z: 4, core: 2. Of those that a mesh axis runs over, the one named last changes fastest.
Arguments:
- inputs: float32 [16384, 768], P(('fsdp', 'tensor')), may hold values from -10 to 10
- qkv_weight: bfloat16 [3, 768, 768], P(None, 'fsdp', 'tensor'), may hold values from -0.21875 to 0.21875
- out_weight: bfloat16 [768, 768], P('tensor', 'fsdp'), may hold values from -0.4375 to 0.4375
- conv_weight: float32 [12, 33], replicated, may hold values from -1 to 1
- up_weight: bfloat16 [768, 3072], P('fsdp', 'tensor'), may hold values from -0.21875 to 0.21875
- down_weight: bfloat16 [3072, 768], P('tensor', 'fsdp'), may hold values from -0.109375 to 0.109375
- mix_gain: float32 [768], replicated, may hold values from 0.25 to 1.75
- mix_bias: float32 [768], replicated, may hold values from -1.2 to 1.2
- feed_gain: float32 [768], replicated, may hold values from 0.25 to 1.75
- feed_bias: float32 [768], replicated, may hold values from -1.2 to 1.2
- out_grad: float32 [16384, 768], P(('fsdp', 'tensor')), may hold values from -6 to 6
Outputs:
- output: float32 [16384, 768], P(('fsdp', 'tensor'))
- input_grad: float32 [16384, 768], P(('fsdp', 'tensor'))
- qkv_grad: float32 [3, 768, 768], P(None, 'fsdp', 'tensor')
- out_weight_grad: float32 [768, 768], P('tensor', 'fsdp')
- conv_grad: float32 [12, 33], replicated
- up_grad: float32 [768, 3072], P('fsdp', 'tensor')
- down_grad: float32 [3072, 768], P('tensor', 'fsdp')
- mix_gain_grad: float32 [768], replicated
- mix_bias_grad: float32 [768], replicated
- feed_gain_grad: float32 [768], replicated
- feed_bias_grad: float32 [768], replicated
All inputs are finite; a program needn't handle non-finite values.
Results may differ from a plain program's by a relative error of at most 0.014.
Values may be sent and summed in bfloat16 or wider, within the bound.
No kernel may reach another device: no remote copies, remote signals or barrier semaphores. Data moves between devices by JAX's collectives and lax.ppermute only.
A program may use at most 192 MiB of HBM per device.

v0:
```python
import jax
import jax.numpy as jnp
from jax import lax
from jax.sharding import PartitionSpec as P

HD = 64
LANDMARKS = 64
ITERS = 6


def in_blocks(value, dim, count):
    lengths = value.shape
    tiles = value.reshape(*lengths[:dim], count, lengths[dim] // count, *lengths[dim + 1 :])
    return jnp.moveaxis(tiles, dim, 0)


def sum_at_owner(value, axis, dim):
    tiles = in_blocks(value, dim, lax.axis_size(axis))
    arrived = lax.all_to_all(tiles, axis, split_axis=0, concat_axis=0, tiled=True)
    return arrived.astype(jnp.float32).sum(axis=0)


def landmarks(query, key):
    heads, length, width = query.shape
    factor = width ** (-0.25)
    scaled_q = query * factor
    scaled_k = key * factor
    marks_q = jnp.mean(scaled_q.reshape(heads, LANDMARKS, length // LANDMARKS, width), axis=2)
    marks_k = jnp.mean(scaled_k.reshape(heads, LANDMARKS, length // LANDMARKS, width), axis=2)
    inner = jnp.einsum("hid,hjd->hij", marks_q, marks_k, precision=lax.Precision.HIGHEST)
    kernel_two = jax.nn.softmax(inner, axis=-1)
    return (scaled_q, scaled_k, marks_q, marks_k, kernel_two)


def column_peak(query, key):
    kernel_two = landmarks(query, key)[4]
    return jnp.max(jnp.sum(kernel_two, axis=1), axis=1)


def mixing(query, key, value, conv, inverse):
    high = lax.Precision.HIGHEST
    scaled_q, scaled_k, marks_q, marks_k, kernel_two = landmarks(query, key)
    length = query.shape[1]
    kernel_one = jax.nn.softmax(
        jnp.einsum("hnd,hjd->hnj", scaled_q, marks_k, precision=high), axis=-1
    )
    kernel_three = jax.nn.softmax(
        jnp.einsum("hid,hnd->hin", marks_q, scaled_k, precision=high), axis=-1
    )
    approx = jnp.swapaxes(kernel_two, 1, 2) * inverse[:, None, None]
    ident = jnp.eye(kernel_two.shape[1], dtype=jnp.float32)
    for step in range(ITERS):
        prod = jnp.einsum("hij,hjk->hik", kernel_two, approx, precision=high)
        inner = 7.0 * ident - prod
        inner = 15.0 * ident - jnp.einsum("hij,hjk->hik", prod, inner, precision=high)
        inner = 13.0 * ident - jnp.einsum("hij,hjk->hik", prod, inner, precision=high)
        approx = jnp.einsum("hij,hjk->hik", 0.25 * approx, inner, precision=high)
    summary = jnp.einsum("hin,hnd->hid", kernel_three, value, precision=high)
    carried = jnp.einsum("hij,hjd->hid", approx, summary, precision=high)
    mixed = jnp.einsum("hnj,hjd->hnd", kernel_one, carried, precision=high)
    margin = conv.shape[1] // 2
    padded = jnp.pad(value, ((0, 0), (margin, margin), (0, 0)))
    for tap in range(conv.shape[1]):
        mixed = mixed + conv[:, tap][:, None, None] * padded[:, tap : tap + length, :]
    return mixed


def gelu_tanh(value):
    return jax.nn.gelu(value, approximate=True)


def norm_forward(rows, gain, shift):
    center = rows - jnp.mean(rows, axis=-1, keepdims=True)
    spread = jnp.mean(center * center, axis=-1, keepdims=True)
    factor = lax.rsqrt(spread + 1e-05)
    normed = center * factor
    return (normed * gain + shift, normed, factor)


def norm_backward(cotan, normed, factor, gain):
    scaled = cotan * gain
    return factor * (
        scaled
        - jnp.mean(scaled, axis=-1, keepdims=True)
        - normed * jnp.mean(scaled * normed, axis=-1, keepdims=True)
    )


def norm_params(cotan, normed):
    return (jnp.sum(cotan * normed, axis=0), jnp.sum(cotan, axis=0))


def shards(
    inputs,
    qkv_weight,
    out_weight,
    conv_weight,
    up_weight,
    down_weight,
    mix_gain,
    mix_bias,
    feed_gain,
    feed_bias,
    out_grad,
):
    place = lax.axis_index("tensor")
    gathered_in = lax.all_gather(inputs.astype(jnp.bfloat16), "tensor", axis=0, tiled=True)
    length = gathered_in.shape[0]
    w_qkv, w_out, w_up, w_down = (
        lax.all_gather(qkv_weight, "fsdp", axis=1, tiled=True),
        lax.all_gather(out_weight, "fsdp", axis=1, tiled=True),
        lax.all_gather(up_weight, "fsdp", axis=0, tiled=True),
        lax.all_gather(down_weight, "fsdp", axis=1, tiled=True),
    )
    columns = w_qkv.shape[2]
    local_heads = columns // HD
    qkv = jnp.einsum("nd,kdc->knc", gathered_in, w_qkv, preferred_element_type=jnp.float32)

    def split_heads(block):
        return block.reshape(length, local_heads, HD).transpose(1, 0, 2)

    query, key, value = (split_heads(qkv[0]), split_heads(qkv[1]), split_heads(qkv[2]))
    conv_local = lax.dynamic_slice_in_dim(conv_weight, place * local_heads, local_heads, 0)
    peak_local = column_peak(query, key)
    peak = lax.pmax(peak_local, "fsdp")
    inverse = 1.0 / peak
    mixed, mixing_back = jax.vjp(mixing, query, key, value, conv_local, inverse)
    context = mixed.transpose(1, 0, 2).reshape(length, columns).astype(jnp.bfloat16)
    attended = lax.psum_scatter(
        jnp.dot(context, w_out, preferred_element_type=jnp.float32),
        "tensor",
        scatter_dimension=0,
        tiled=True,
    )
    mixed_rows, normed_mix, factor_mix = norm_forward(inputs + attended, mix_gain, mix_bias)
    mixed_low = lax.all_gather(mixed_rows.astype(jnp.bfloat16), "tensor", axis=0, tiled=True)
    up_rows = jnp.dot(mixed_low, w_up, preferred_element_type=jnp.float32)
    act, gelu_back = jax.vjp(gelu_tanh, up_rows)
    act_low = act.astype(jnp.bfloat16)
    fed = lax.psum_scatter(
        jnp.dot(act_low, w_down, preferred_element_type=jnp.float32).astype(jnp.bfloat16),
        "tensor",
        scatter_dimension=0,
        tiled=True,
    ).astype(jnp.float32)
    output, normed_feed, factor_feed = norm_forward(mixed_rows + fed, feed_gain, feed_bias)
    grad_feed = norm_backward(out_grad, normed_feed, factor_feed, feed_gain)
    feed_gain_part, feed_bias_part = norm_params(out_grad, normed_feed)
    grad_down = lax.all_gather(grad_feed.astype(jnp.bfloat16), "tensor", axis=0, tiled=True)
    down_grad = jnp.einsum("nf,nd->fd", act_low, grad_down, preferred_element_type=jnp.float32)
    grad_act = jnp.einsum("nd,fd->nf", grad_down, w_down, preferred_element_type=jnp.float32)
    grad_up = gelu_back(grad_act)[0].astype(jnp.bfloat16)
    up_grad = jnp.einsum("nd,nf->df", mixed_low, grad_up, preferred_element_type=jnp.float32)
    grad_mixed_rows = grad_feed + lax.psum_scatter(
        jnp.einsum("nf,df->nd", grad_up, w_up, preferred_element_type=jnp.float32).astype(
            jnp.bfloat16
        ),
        "tensor",
        scatter_dimension=0,
        tiled=True,
    ).astype(jnp.float32)
    grad_mix = norm_backward(grad_mixed_rows, normed_mix, factor_mix, mix_gain)
    mix_gain_part, mix_bias_part = norm_params(grad_mixed_rows, normed_mix)
    grad_attended = lax.all_gather(grad_mix.astype(jnp.bfloat16), "tensor", axis=0, tiled=True)
    out_weight_grad = jnp.einsum(
        "nc,nd->cd", context, grad_attended, preferred_element_type=jnp.float32
    )
    grad_context = jnp.einsum("nd,cd->nc", grad_attended, w_out, preferred_element_type=jnp.float32)
    grad_mixed = grad_context.reshape(length, local_heads, HD).transpose(1, 0, 2)
    grad_query, grad_key, grad_value, grad_conv, grad_inverse = mixing_back(grad_mixed)
    grad_peak = -grad_inverse * inverse * inverse
    head_total = conv_weight.shape[0]
    peak_full = lax.dynamic_update_slice_in_dim(
        jnp.zeros((head_total,), jnp.float32), grad_peak, place * local_heads, 0
    )
    conv_full = lax.dynamic_update_slice_in_dim(
        jnp.zeros(conv_weight.shape, jnp.float32), grad_conv, place * local_heads, 0
    )
    norm_stack = jnp.stack([mix_gain_part, mix_bias_part, feed_gain_part, feed_bias_part])
    peak_sum, conv_grad, norm_sum = lax.psum((peak_full, conv_full, norm_stack), ("fsdp", "tensor"))
    peak_total = lax.dynamic_slice_in_dim(peak_sum, place * local_heads, local_heads, 0)
    owner = jnp.where(peak_local == peak, peak_total, 0.0)
    unused, peak_back = jax.vjp(column_peak, query, key)
    extra_query, extra_key = peak_back(owner)

    def merge_heads(block):
        return block.transpose(1, 0, 2).reshape(length, columns)

    grad_qkv = jnp.stack(
        [
            merge_heads(grad_query + extra_query),
            merge_heads(grad_key + extra_key),
            merge_heads(grad_value),
        ]
    ).astype(jnp.bfloat16)
    qkv_grad = jnp.einsum("nd,knc->kdc", gathered_in, grad_qkv, preferred_element_type=jnp.float32)
    input_grad = grad_mix + lax.psum_scatter(
        jnp.einsum("knc,kdc->nd", grad_qkv, w_qkv, preferred_element_type=jnp.float32).astype(
            jnp.bfloat16
        ),
        "tensor",
        scatter_dimension=0,
        tiled=True,
    ).astype(jnp.float32)
    qkv_share, out_share, up_share, down_share = (
        sum_at_owner(qkv_grad.astype(jnp.bfloat16), "fsdp", 1),
        sum_at_owner(out_weight_grad.astype(jnp.bfloat16), "fsdp", 1),
        sum_at_owner(up_grad.astype(jnp.bfloat16), "fsdp", 0),
        sum_at_owner(down_grad.astype(jnp.bfloat16), "fsdp", 1),
    )
    return (
        output,
        input_grad,
        qkv_share,
        out_share,
        conv_grad,
        up_share,
        down_share,
        norm_sum[0],
        norm_sum[1],
        norm_sum[2],
        norm_sum[3],
    )


def solution(mesh):
    placed = (
        P(("fsdp", "tensor"), None),
        P(None, "fsdp", "tensor"),
        P("tensor", "fsdp"),
        P(),
        P("fsdp", "tensor"),
        P("tensor", "fsdp"),
        P(),
        P(),
        P(),
        P(),
        P(("fsdp", "tensor"), None),
    )
    return jax.shard_map(
        shards,
        mesh=mesh,
        in_specs=placed,
        out_specs=(
            P(("fsdp", "tensor"), None),
            P(("fsdp", "tensor"), None),
            P(None, "fsdp", "tensor"),
            P("tensor", "fsdp"),
            P(),
            P("fsdp", "tensor"),
            P("tensor", "fsdp"),
            P(),
            P(),
            P(),
            P(),
        ),
        check_vma=False,
    )
```

profile of v0, /device:TPU:0, one launch (start us, length us, event | category | flops | bytes accessed | tf_op | source)
XLA Modules:
  0.0 735.5 jit_solution(5595995136005372708)
XLA Ops:
  12.9 35.1 %all_gather.26 = bf16[192,768]{0,1:T(8,128)(2,1)} all-gather(bf16[192,96]{0,1:T(8,128)(2,1)S(1)} %copy.111), channel_id=1, replica_groups=mesh['fsdp'=8,'tensor'=4] {'fsdp'}, dimensions={1}, use_global_device_ids=true | all-gather | bytes 331776 | tf_op jit(solution)/shard_map/all_gather | solution.py:111
  48.0 38.3 %all_gather.24 = bf16[3,768,192]{2,0,1:T(4,128)(2,1)S(1)} all-gather(bf16[3,96,192]{2,0,1:T(4,128)(2,1)S(1)} %copy.100), channel_id=1, replica_groups=mesh['fsdp'=8,'tensor'=4] {'fsdp'}, dimensions={1}, use_global_device_ids=true | all-gather | bytes 995328 | tf_op jit(solution)/shard_map/all_gather | solution.py:110
  87.5 4.6 convolution_bitcast_fusion
  96.3 3.3 copy.103
  99.6 4.4 bitcast_reduce_fusion
  104.0 2.6 fusion.116
  107.3 2.9 fusion.124
  110.2 19.7 %pmax.7 = f32[3]{0:T(128)S(1)} all-reduce(f32[3]{0:T(128)S(1)} %reduce_max.37), channel_id=1, replica_groups=mesh['fsdp'=8,'tensor'=4] {'fsdp'}, use_global_device_ids=true, to_apply=%region_8.0 | all-reduce | flops 3 | bytes 24 | tf_op jit(solution)/shard_map/pmax | solution.py:125
  145.2 14.7 %fusion.56 = bf16[3,2048,64]{1,2,0:T(8,128)(2,1)S(1)} fusion(f32[3,64,64]{2,1,0:T(8,128)S(1)} %fusion.210, f32[3,2048,64]{1,2,0:T(8,128)S(1)} %bitcast.257, f32[3]{0:T(128)S(1)} %copy-done.126, f32[3]{0:T(128)S(1)} %copy-done.138, f32[3]{0:T(128)S(1)} %copy-done.139, f32[3]{0:T(128)S(1)} %copy-done.140, f32[3]{0:T(128)S(1)} %copy-done.141, ...), kind=kOutput, calls=%fused_computation.69 | convolution fusion | flops 328728576 | bytes 4006284 | tf_op jit(solution)/shard_map/jvp(hnj,hjd->hnd)/dot_general | solution.py:60
  160.8 3.7 fusion.211
  165.2 55.7 %reduce-scatter.5.cloned.1.call-done = f32[512,768]{1,0:T(8,128)} async-done(((f32[2048,768]{1,0:T(8,128)}), f32[512,768]{1,0:T(8,128)}) %reduce-scatter.5.cloned.1.call-update) | async-done | bytes 1572880 | tf_op jit(solution)/shard_map/reduce_scatter | solution.py:129
  225.6 27.8 %all-gather.9.cloned.1.call-done = bf16[2048,768]{1,0:T(8,128)(2,1)} async-done(((bf16[512,768]{1,0:T(8,128)(2,1)}), bf16[2048,768]{1,0:T(8,128)(2,1)}) %all-gather.9.cloned.1.call-update) | async-done | bytes 3145744 | tf_op jit(solution)/shard_map/all_gather | solution.py:136
  253.4 7.5 %fusion.212 = f32[2048,768]{1,0:T(8,128)} fusion(bf16[2048,768]{1,0:T(8,128)(2,1)} %all-gather.9.cloned.1.call-done, bf16[768,768]{1,0:T(8,128)(2,1)} %all-gather.11.cloned.1.call-done), kind=kOutput, calls=%fused_computation.447 | convolution fusion | flops 2415919104 | bytes 10616832 | tf_op jit(solution)/shard_map/dot_general | solution.py:137
  260.9 36.0 %all-gather.13.cloned.1.call-done = bf16[768,768]{0,1:T(8,128)(2,1)} async-done(((bf16[768,96]{0,1:T(8,128)(2,1)}), bf16[768,768]{0,1:T(8,128)(2,1)}) %all-gather.13.cloned.1.call-update) | async-done | bytes 1179664 | tf_op jit(solution)/shard_map/all_gather | solution.py:113
  296.9 8.6 %convolution_convert_fusion.1 = bf16[2048,768]{1,0:T(8,128)(2,1)} fusion(bf16[768,768]{0,1:T(8,128)(2,1)} %all-gather.13.cloned.1.call-done, f32[2048,768]{1,0:T(8,128)} %fusion.212), kind=kOutput, calls=%fused_computation.15 | convolution fusion | flops 2431647744 | bytes 10616832 | tf_op jit(solution)/shard_map/dot_general | solution.py:141
  305.6 36.1 %reduce-scatter.7.cloned.1.call-done = bf16[512,768]{1,0:T(8,128)(2,1)} async-done(((bf16[2048,768]{1,0:T(8,128)(2,1)}), bf16[512,768]{1,0:T(8,128)(2,1)}) %reduce-scatter.7.cloned.1.call-update) | async-done | bytes 786448 | tf_op jit(solution)/shard_map/reduce_scatter | solution.py:140
  348.3 28.4 %all-gather.15.cloned.1.call-done = bf16[2048,768]{1,0:T(8,128)(2,1)} async-done(((bf16[512,768]{1,0:T(8,128)(2,1)}), bf16[2048,768]{1,0:T(8,128)(2,1)}) %all-gather.15.cloned.1.call-update) | async-done | bytes 3145744 | tf_op jit(solution)/shard_map/all_gather | solution.py:149
  376.7 8.5 %fusion.9 = bf16[2048,768]{1,0:T(8,128)(2,1)S(1)} fusion(f32[2048,768]{1,0:T(8,128)} %fusion.212, bf16[2048,768]{1,0:T(8,128)(2,1)} %all-gather.15.cloned.1.call-done, bf16[768,768]{0,1:T(8,128)(2,1)} %all-gather.13.cloned.1.call-done), kind=kOutput, calls=%fused_computation.11 | convolution fusion | flops 2447376384 | bytes 13762560 | tf_op jit(solution)/shard_map/nd,fd->nf/dot_general | solution.py:151
  386.9 4.0 convolution_convert_fusion
  391.0 38.0 %reduce-scatter.9.cloned.1.call-done = bf16[512,768]{1,0:T(8,128)(2,1)} async-done(((bf16[2048,768]{1,0:T(8,128)(2,1)}), bf16[512,768]{1,0:T(8,128)(2,1)}) %reduce-scatter.9.cloned.1.call-update) | async-done | bytes 786448 | tf_op jit(solution)/shard_map/reduce_scatter | solution.py:154
  429.0 3.1 multiply_reduce_fusion.1
  436.8 8.0 %convolution_convert_fusion.2 = bf16[768,768]{0,1:T(8,128)(2,1)} fusion(bf16[2048,768]{1,0:T(8,128)(2,1)} %all-gather.15.cloned.1.call-done, f32[2048,768]{1,0:T(8,128)} %fusion.212), kind=kOutput, calls=%fused_computation.133 | convolution fusion | flops 2430664704 | bytes 10616832 | tf_op jit(solution)/shard_map/nf,nd->fd/dot_general | solution.py:150
  444.7 5.5 all-to-all-start.3
  450.4 12.3 %all-gather.17.cloned.1.call-done = bf16[2048,768]{1,0:T(8,128)(2,1)} async-done(((bf16[512,768]{1,0:T(8,128)(2,1)}), bf16[2048,768]{1,0:T(8,128)(2,1)}) %all-gather.17.cloned.1.call-update) | async-done | bytes 3145744 | tf_op jit(solution)/shard_map/all_gather | solution.py:164
  462.7 3.1 fusion.213
  465.8 8.2 %multiply_reduce_fusion.34 = (f32[3]{0:T(128)S(1)}, f32[3]{0:T(128)S(1)}, f32[3]{0:T(128)S(1)}, f32[3]{0:T(128)S(1)}, f32[3]{0:T(128)S(1)}, /*index=5*/f32[3]{0:...) fusion(f32[3,2048,64]{1,2,0:T(8,128)S(1)} %bitcast.250, ...), kind=kLoop, calls=%fused_computation.117 | loop fusion | flops 14155722 | bytes 3145944 | tf_op jit(solution)/shard_map/transpose(jvp())/reduce_sum | solution.py:64
  489.6 7.8 %multiply_reduce_fusion.33 = (f32[3]{0:T(128)S(1)}, f32[3]{0:T(128)S(1)}, f32[3]{0:T(128)S(1)}, f32[3]{0:T(128)S(1)}, f32[3]{0:T(128)S(1)}, /*index=5*/f32[3]{0:...) fusion(f32[3,2048,64]{1,2,0:T(8,128)S(1)} %bitcast.252, ...), kind=kLoop, calls=%fused_computation.116 | loop fusion | flops 12976083 | bytes 7864536 | tf_op jit(solution)/shard_map/transpose(jvp())/reduce_sum | solution.py:64
  504.5 40.0 %all-reduce.67 = (f32[12]{0:T(128)S(1)}, f32[12,33]{1,0:T(8,128)}, f32[4,768]{1,0:T(4,128)}) all-reduce(f32[12]{0:T(128)S(1)} %fusion.168, f32[12,33]{1,0:T(8,128)S(1)} %dynamic_update_slice.7, f32[4,768]{1,0:T(4,128)S(1)} %pad_maximum_fusion.3), channel_id=1, replica_groups=mesh['fsdp'=8,'tensor'=4] {'fsdp','tensor'}, use_global_device_ids=true, to_apply=%region_26.27 | all-reduce | flops 3480 | bytes 27840 | tf_op jit(solution)/shard_map/psum | solution.py:180
  549.8 7.4 %broadcast_multiply_fusion.1 = (f32[3,2048,64]{1,2,0:T(8,128)}, f32[3,2048,64]{1,2,0:T(8,128)}, f32[3,2048,64]{1,2,0:T(8,128)}, f32[3,2048,64]{1,2,0:T(8,128)}, ...) fusion(f32[3,2048,64]{1,2,0:T(8,128)S(1)} %bitcast.253, ...), kind=kLoop, calls=%fused_computation.216 | loop fusion | flops 4718592 | bytes 20447376 | tf_op jit(solution)/shard_map/transpose(jvp())/mul | solution.py:64
  557.4 11.1 %broadcast_multiply_fusion = (f32[3,2048,64]{1,2,0:T(8,128)}, f32[3,2048,64]{1,2,0:T(8,128)}, f32[3,2048,64]{1,2,0:T(8,128)}, f32[3,2048,64]{1,2,0:T(8,128)}, f3...) fusion(f32[3,2048,64]{1,2,0:T(8,128)S(1)} %bitcast.254, ...), kind=kLoop, calls=%fused_computation.215 | loop fusion | flops 7077888 | bytes 29884632 | tf_op jit(solution)/shard_map/transpose(jvp())/mul | solution.py:64
  578.3 3.4 copy.136
  583.7 3.2 copy.139
  588.7 3.3 copy.134
  593.9 3.3 copy.138
  597.2 5.2 fusion.54
  602.5 2.9 fusion.55
  605.5 18.7 %pad_add_fusion = f32[3,2080,64]{1,2,0:T(8,128)S(1)} fusion(f32[3,2048,64]{1,2,0:T(8,128)S(1)} %copy-done.10, f32[3,2048,64]{1,2,0:T(8,128)S(1)} %copy-done.11, f32[3,2048,64]{1,2,0:T(8,128)S(1)} %copy-done.12, f32[3,2048,64]{1,2,0:T(8,128)} %get-tuple-element.129, f32[3,2048,64]{1,2,0:T(8,128)} %get-tuple-element.130, ...), kind=kLoop, calls=%fused_computation.74 | loop fusion | flops 10383360 | bytes 44064768 | tf_op jit(solution)/shard_map/transpose(jvp())/add_any | solution.py:64
  624.2 7.5 %fusion.53 = bf16[3,2048,64]{1,2,0:T(8,128)(2,1)S(1)} fusion(f32[3,64,64]{2,1,0:T(8,128)S(1)} %copy-done.52, f32[3,2048,64]{1,2,0:T(8,128)} %get-tuple-element.119, f32[3,2048,64]{1,2,0:T(8,128)} %get-tuple-element.120, f32[3,2048,64]{1,2,0:T(8,128)} %get-tuple-element.121, f32[3,2048,64]{1,2,0:T(8,128)} %get-tuple-element.123, ...), kind=kOutput, calls=%fused_computation.66 | convolution fusion | flops 305528832 | bytes 13419264 | tf_op jit(solution)/shard_map/transpose(jvp(hin,hnd->hid))/dot_general | solution.py:58
  632.6 4.2 bitcast_convert_fusion
  636.8 6.5 convolution_convert_fusion.3
  643.3 5.4 all-to-all-start.2
  648.7 2.7 convolution_convert_fusion.4
  652.7 24.3 %all-to-all-done.2 = bf16[8,96,768]{2,1,0:T(8,128)(2,1)S(1)} async-done(((bf16[8,96,768]{2,1,0:T(8,128)(2,1)}), bf16[8,96,768]{2,1,0:T(8,128)(2,1)S(1)}, u32[]{:S(2)}, u32[]{:S(2)}) %all-to-all-start.2) | async-done | bytes 1179680 | tf_op jit(solution)/shard_map/all_to_all | solution.py:19
  677.0 3.5 all-to-all-start.1
  680.5 5.0 fusion.61
  689.2 3.1 all-to-all-done.1
  692.4 3.6 all-to-all-start
  700.4 24.3 %all-to-all-done = bf16[8,3,96,192]{2,3,1,0:T(8,128)(2,1)S(1)} async-done(((bf16[8,3,96,192]{2,3,1,0:T(8,128)(2,1)}), bf16[8,3,96,192]{2,3,1,0:T(8,128)(2,1)S(1)}, u32[]{:S(2)}, u32[]{:S(2)}) %all-to-all-start) | async-done | bytes 884768 | tf_op jit(solution)/shard_map/all_to_all | solution.py:19
  (506 shorter events, 100.2 us)
Async XLA Ops:
  8.0 78.3 %all-gather.7.cloned.1.call-start = ((), (), s32[]{:S(2)}) async-start(), calls=%async_computation.8 | async-start | bytes 3932160 | tf_op jit(solution)/shard_map/all_gather | solution.py:107
  10.5 210.4 %reduce-scatter.5.cloned.1.call-start = ((), (), s32[]{:S(2)}) async-start(), calls=%async_computation.9 | async-start | bytes 7864320 | tf_op jit(solution)/shard_map/reduce_scatter | solution.py:129
  11.8 133.1 %copy-start.102 = (f32[3]{0:T(128)}, f32[3]{0:T(128)S(1)}, u32[]{:S(2)}) copy-start(f32[3]{0:T(128)S(1)} %get-tuple-element.89) | copy-start | bytes 40
  11.8 133.1 %copy-start.104 = (f32[3]{0:T(128)}, f32[3]{0:T(128)S(1)}, u32[]{:S(2)}) copy-start(f32[3]{0:T(128)S(1)} %get-tuple-element.90) | copy-start | bytes 40
  93.9 10.0 %copy-start.2 = (f32[1,2048,192]{1,2,0:T(8,128)}, f32[1,2048,192]{1,2,0:T(8,128)S(1)}, u32[]{:S(2)}) copy-start(f32[1,2048,192]{1,2,0:T(8,128)S(1)} %get-tuple-element.116) | copy-start | bytes 4718596
  139.9 296.2 %copy-start.91 = (f32[3,64]{1,0:T(4,128)}, f32[3,64]{1,0:T(4,128)S(1)}, u32[]{:S(2)}) copy-start(f32[3,64]{1,0:T(4,128)S(1)} %get-tuple-element.154) | copy-start | bytes 2308
  144.5 15.4 %copy-start.85 = (f32[3,64,64]{2,1,0:T(8,128)}, f32[3,64,64]{2,1,0:T(8,128)S(1)}, u32[]{:S(2)}) copy-start(f32[3,64,64]{2,1,0:T(8,128)S(1)} %fusion.210) | copy-start | bytes 147460
  145.2 15.6 %copy-start.22 = (bf16[192,768]{0,1:T(8,128)(2,1)S(1)}, bf16[192,768]{0,1:T(8,128)(2,1)}, u32[]{:S(2)}) copy-start(bf16[192,768]{0,1:T(8,128)(2,1)} %all_gather.26) | copy-start | bytes 884740
  164.6 61.0 %all-gather.11.cloned.1.call-start = ((), (), s32[]{:S(2)}) async-start(), calls=%async_computation.11 | async-start | bytes 1327104 | tf_op jit(solution)/shard_map/all_gather | solution.py:112
  165.1 88.3 %all-gather.9.cloned.1.call-start = ((), (), s32[]{:S(2)}) async-start(), calls=%async_computation.10 | async-start | bytes 3932160 | tf_op jit(solution)/shard_map/all_gather | solution.py:136
  224.9 72.0 %all-gather.13.cloned.1.call-start = ((), (), s32[]{:S(2)}) async-start(), calls=%async_computation.12 | async-start | bytes 1327104 | tf_op jit(solution)/shard_map/all_gather | solution.py:113
  225.5 116.2 %reduce-scatter.7.cloned.1.call-start = ((), (), s32[]{:S(2)}) async-start(), calls=%async_computation.13 | async-start | bytes 3932160 | tf_op jit(solution)/shard_map/reduce_scatter | solution.py:140
  305.5 71.2 %all-gather.15.cloned.1.call-start = ((), (), s32[]{:S(2)}) async-start(), calls=%async_computation.14 | async-start | bytes 3932160 | tf_op jit(solution)/shard_map/all_gather | solution.py:149
  348.2 80.8 %reduce-scatter.9.cloned.1.call-start = ((), (), s32[]{:S(2)}) async-start(), calls=%async_computation.15 | async-start | bytes 3932160 | tf_op jit(solution)/shard_map/reduce_scatter | solution.py:154
  376.7 10.2 %copy-start.157 = (bf16[768,768]{1,0:T(8,128)(2,1)S(1)}, bf16[768,768]{1,0:T(8,128)(2,1)}, u32[]{:S(2)}) copy-start(bf16[768,768]{1,0:T(8,128)(2,1)} %all-gather.11.cloned.1.call-done) | copy-start | bytes 3538948
  390.9 71.8 %all-gather.17.cloned.1.call-start = ((), (), s32[]{:S(2)}) async-start(), calls=%async_computation.16 | async-start | bytes 3932160 | tf_op jit(solution)/shard_map/all_gather | solution.py:164
  444.7 198.6 %all-to-all-start.3 = ((bf16[8,768,96]{1,2,0:T(8,128)(2,1)}), bf16[8,768,96]{1,2,0:T(8,128)(2,1)}, u32[]{:S(2)}, u32[]{:S(2)}) async-start(bf16[8,768,96]{1,2,0:T(8,128)(2,1)} %bitcast.70), calls=%async_computation.7 | async-start | bytes 2359296 | tf_op jit(solution)/shard_map/all_to_all | solution.py:19
  450.3 275.5 %reduce-scatter.11.cloned.1.call-start = ((), (), s32[]{:S(2)}) async-start(), calls=%async_computation.17 | async-start | bytes 3932160 | tf_op jit(solution)/shard_map/reduce_scatter | solution.py:197
  465.8 8.2 %copy-start.15 = (f32[3,2048,64]{1,2,0:T(8,128)S(1)}, f32[3,2048,64]{1,2,0:T(8,128)}, u32[]{:S(2)}) copy-start(f32[3,2048,64]{1,2,0:T(8,128)} %copy-done.14) | copy-start | bytes 4718596
  498.3 49.1 %copy-start.35 = (f32[3,64,64]{2,1,0:T(8,128)S(1)}, f32[3,64,64]{2,1,0:T(8,128)}, u32[]{:S(2)}) copy-start(f32[3,64,64]{2,1,0:T(8,128)} %copy-done.34) | copy-start | bytes 147460
  504.5 65.8 %copy-start.51 = (f32[3,64,64]{2,1,0:T(8,128)}, f32[3,64,64]{2,1,0:T(8,128)S(1)}, u32[]{:S(2)}) copy-start(f32[3,64,64]{2,1,0:T(8,128)S(1)} %fusion.214) | copy-start | bytes 147460
  549.6 7.6 %copy-start.103 = (f32[3]{0:T(128)S(1)}, f32[3]{0:T(128)}, u32[]{:S(2)}) copy-start(f32[3]{0:T(128)} %copy-done.102) | copy-start | bytes 40
  549.7 7.6 %copy-start.105 = (f32[3]{0:T(128)S(1)}, f32[3]{0:T(128)}, u32[]{:S(2)}) copy-start(f32[3]{0:T(128)} %copy-done.104) | copy-start | bytes 40
  549.7 7.6 %copy-start.107 = (f32[3]{0:T(128)S(1)}, f32[3]{0:T(128)}, u32[]{:S(2)}) copy-start(f32[3]{0:T(128)} %get-tuple-element.91) | copy-start | bytes 40
  549.7 7.6 %copy-start.109 = (f32[3]{0:T(128)S(1)}, f32[3]{0:T(128)}, u32[]{:S(2)}) copy-start(f32[3]{0:T(128)} %get-tuple-element.92) | copy-start | bytes 40
  549.7 7.6 %copy-start.111 = (f32[3]{0:T(128)S(1)}, f32[3]{0:T(128)}, u32[]{:S(2)}) copy-start(f32[3]{0:T(128)} %get-tuple-element.93) | copy-start | bytes 40
  549.7 7.6 %copy-start.113 = (f32[3]{0:T(128)S(1)}, f32[3]{0:T(128)}, u32[]{:S(2)}) copy-start(f32[3]{0:T(128)} %get-tuple-element.94) | copy-start | bytes 40
  549.7 7.6 %copy-start.115 = (f32[3]{0:T(128)S(1)}, f32[3]{0:T(128)}, u32[]{:S(2)}) copy-start(f32[3]{0:T(128)} %get-tuple-element.95) | copy-start | bytes 40
  549.7 7.6 %copy-start.117 = (f32[3]{0:T(128)S(1)}, f32[3]{0:T(128)}, u32[]{:S(2)}) copy-start(f32[3]{0:T(128)} %get-tuple-element.96) | copy-start | bytes 40
  549.7 7.6 %copy-start.119 = (f32[3]{0:T(128)S(1)}, f32[3]{0:T(128)}, u32[]{:S(2)}) copy-start(f32[3]{0:T(128)} %get-tuple-element.97) | copy-start | bytes 40
  549.7 7.6 %copy-start.121 = (f32[3]{0:T(128)S(1)}, f32[3]{0:T(128)}, u32[]{:S(2)}) copy-start(f32[3]{0:T(128)} %get-tuple-element.98) | copy-start | bytes 40
  549.7 7.6 %copy-start.123 = (f32[3]{0:T(128)S(1)}, f32[3]{0:T(128)}, u32[]{:S(2)}) copy-start(f32[3]{0:T(128)} %get-tuple-element.99) | copy-start | bytes 40
  549.8 7.6 %copy-start.125 = (f32[3]{0:T(128)S(1)}, f32[3]{0:T(128)}, u32[]{:S(2)}) copy-start(f32[3]{0:T(128)} %get-tuple-element.100) | copy-start | bytes 40
  549.8 7.6 %copy-start.127 = (f32[3]{0:T(128)S(1)}, f32[3]{0:T(128)}, u32[]{:S(2)}) copy-start(f32[3]{0:T(128)} %get-tuple-element.70) | copy-start | bytes 40
  549.8 7.6 %copy-start.129 = (f32[3]{0:T(128)S(1)}, f32[3]{0:T(128)}, u32[]{:S(2)}) copy-start(f32[3]{0:T(128)} %get-tuple-element.83) | copy-start | bytes 40
  549.8 7.6 %copy-start.131 = (f32[3]{0:T(128)S(1)}, f32[3]{0:T(128)}, u32[]{:S(2)}) copy-start(f32[3]{0:T(128)} %get-tuple-element.84) | copy-start | bytes 40
  557.4 11.2 %copy-start.16 = (f32[3,2048,64]{1,2,0:T(8,128)S(1)}, f32[3,2048,64]{1,2,0:T(8,128)}, u32[]{:S(2)}) copy-start(f32[3,2048,64]{1,2,0:T(8,128)} %copy-done.14) | copy-start | bytes 4718596
  557.4 11.2 %copy-start.86 = (f32[3,64,64]{2,1,0:T(8,128)S(1)}, f32[3,64,64]{2,1,0:T(8,128)}, u32[]{:S(2)}) copy-start(f32[3,64,64]{2,1,0:T(8,128)} %copy-done.85) | copy-start | bytes 147460
  605.5 18.7 %copy-start.52 = (f32[3,64,64]{2,1,0:T(8,128)S(1)}, f32[3,64,64]{2,1,0:T(8,128)}, u32[]{:S(2)}) copy-start(f32[3,64,64]{2,1,0:T(8,128)} %copy-done.51) | copy-start | bytes 147460
  624.2 8.4 %copy-start.33 = (bf16[3,768,192]{2,0,1:T(4,128)(2,1)S(1)}, bf16[3,768,192]{2,0,1:T(4,128)(2,1)}, u32[]{:S(2)}) copy-start(bf16[3,768,192]{2,0,1:T(4,128)(2,1)} %copy-done.32) | copy-start | bytes 2654212
  624.2 8.4 %copy-start.158 = (bf16[3,2048,64]{1,2,0:T(8,128)(2,1)S(1)}, bf16[3,2048,64]{1,2,0:T(8,128)(2,1)}, u32[]{:S(2)}) copy-start(bf16[3,2048,64]{1,2,0:T(8,128)(2,1)} %fusion.54) | copy-start | bytes 2359300
  624.2 8.4 %copy-start.160 = (bf16[3,2048,64]{1,2,0:T(8,128)(2,1)S(1)}, bf16[3,2048,64]{1,2,0:T(8,128)(2,1)}, u32[]{:S(2)}) copy-start(bf16[3,2048,64]{1,2,0:T(8,128)(2,1)} %fusion.55) | copy-start | bytes 2359300
  643.3 33.7 %all-to-all-start.2 = ((bf16[8,96,768]{2,1,0:T(8,128)(2,1)}), bf16[8,96,768]{2,1,0:T(8,128)(2,1)S(1)}, u32[]{:S(2)}, u32[]{:S(2)}) async-start(bf16[8,96,768]{2,1,0:T(8,128)(2,1)} %bitcast.273), calls=%async_computation.6 | async-start | bytes 2359296 | tf_op jit(solution)/shard_map/all_to_all | solution.py:19
  651.4 29.1 %copy-start.79 = (bf16[3,2048,64]{1,2,0:T(8,128)(2,1)S(1)}, bf16[3,2048,64]{1,2,0:T(8,128)(2,1)}, u32[]{:S(2)}) copy-start(bf16[3,2048,64]{1,2,0:T(8,128)(2,1)} %copy-done.78) | copy-start | bytes 2359300
  651.8 28.7 %copy-start.159 = (bf16[3,2048,64]{1,2,0:T(8,128)(2,1)S(1)}, bf16[3,2048,64]{1,2,0:T(8,128)(2,1)}, u32[]{:S(2)}) copy-start(bf16[3,2048,64]{1,2,0:T(8,128)(2,1)} %fusion.54) | copy-start | bytes 2359300
  677.0 15.4 %all-to-all-start.1 = ((bf16[8,192,96]{2,1,0:T(8,128)(2,1)}), bf16[8,192,96]{2,1,0:T(8,128)(2,1)S(1)}, u32[]{:S(2)}, u32[]{:S(2)}) async-start(bf16[8,192,96]{2,1,0:T(8,128)(2,1)} %bitcast.249), calls=%async_computation.5 | async-start | bytes 786432 | tf_op jit(solution)/shard_map/all_to_all | solution.py:19
  692.4 32.3 %all-to-all-start = ((bf16[8,3,96,192]{2,3,1,0:T(8,128)(2,1)}), bf16[8,3,96,192]{2,3,1,0:T(8,128)(2,1)S(1)}, u32[]{:S(2)}, u32[]{:S(2)}) async-start(bf16[8,3,96,192]{2,3,1,0:T(8,128)(2,1)} %bitcast.248), calls=%async_computation.4 | async-start | bytes 2359296 | tf_op jit(solution)/shard_map/all_to_all | solution.py:19
  699.0 26.8 %copy-start.19 = (f32[512,768]{1,0:T(8,128)S(1)}, f32[512,768]{1,0:T(8,128)}, u32[]{:S(2)}) copy-start(f32[512,768]{1,0:T(8,128)} %get-tuple-element.108) | copy-start | bytes 4718596
  (130 other events, 342.1 us)
Sparse Core Ops, SparseCore 0:
  11.0 31.2 all-gather.6
  164.7 56.1 reduce-scatter.4
  391.0 37.8 reduce-scatter.8
  636.9 38.9 reduce-scatter.10
Sparse Core Ops, SparseCore 1:
  167.2 38.7 all-gather.10
  225.0 28.3 all-gather.8
  255.5 41.4 all-gather.12
  305.6 36.1 reduce-scatter.6
  348.3 28.3 all-gather.14
  434.3 28.3 all-gather.16
where the time goes:
time: 744 us; the launch traced here: 736 us
  waiting for transfers between devices  287 us (39%)
  matrix products  143 us (19%)
  blocking collectives  133 us (18%)
  other arithmetic  90.6 us (12%)
  local copies, waits for them, and re-layouts  45 us (6%)
  starting transfers between devices  18.5 us (2%)
  between operations  18.4 us (2%)
    reduce_scatter x1, waiting for transfers between devices, shards(): lax.psum_scatter(jnp.dot(context, w_out, preferred_element_type=jnp.float...  55.7 us
    all_to_all x4, waiting for transfers between devices, sum_at_owner(): lax.all_to_all(tiles, axis, split_axis=0, concat_axis=0, tiled=True)  51.7 us
    psum x1, blocking collectives, shards(): lax.psum((peak_full, conv_full, norm_stack), ('fsdp', 'tensor'))  40 us
    all_gather x1, blocking collectives, shards(): lax.all_gather(qkv_weight, 'fsdp', axis=1, tiled=True)  38.3 us
    reduce_scatter x1, waiting for transfers between devices, shards(): lax.psum_scatter(jnp.einsum('nf,df->nd', grad_up, w_up, preferred_element...  38 us
    reduce_scatter x1, waiting for transfers between devices, shards(): lax.psum_scatter(jnp.dot(act_low, w_down, preferred_element_type=jnp.floa...  36.1 us
    all_gather x1, waiting for transfers between devices, shards(): lax.all_gather(down_weight, 'fsdp', axis=1, tiled=True)  36 us
    all_gather x1, blocking collectives, shards(): lax.all_gather(out_weight, 'fsdp', axis=1, tiled=True)  35.1 us
  transfers between devices with their start and end apart: 14, of which 10 were waited for; matrix products, arithmetic and copies ran while one was open for 24% of the time, Pallas kernels for 0%

commit v1 on v0

v1 whole, which is shorter than its diff:
```python
import jax
import jax.numpy as jnp
from jax import lax
from jax.experimental import pallas as pl
from jax.experimental.pallas import tpu as pltpu
from jax.sharding import PartitionSpec as P
HD=64; LANDMARKS=64; ITERS=6
F32=jnp.float32; BF=jnp.bfloat16
SPAN=256; REACH=128

def dot(a,b,ca,cb):
    return lax.dot_general(a,b,(((ca,),(cb,)),((),())),preferred_element_type=F32)

def low(a):
    return a.astype(BF)

def parts(a):
    high=a.astype(BF)
    return high,(a-high.astype(F32)).astype(BF)

def dot3(a,b,ca,cb):
    ah,al=a if isinstance(a,tuple) else parts(a)
    bh,bl=b if isinstance(b,tuple) else parts(b)
    return dot(ah,bh,ca,cb)+(dot(ah,bl,ca,cb)+dot(al,bh,ca,cb))

def segments(length):
    row=lax.broadcasted_iota(jnp.int32,(LANDMARKS,length),0)
    col=lax.broadcasted_iota(jnp.int32,(LANDMARKS,length),1)
    size=length//LANDMARKS
    first=row*size
    return jnp.where((col>=first)&(col<first+size),1.0,0.0).astype(BF)

def soft_rows(s):
    e=jnp.exp(s-jnp.max(s,axis=1,keepdims=True))
    return e*(1.0/jnp.sum(e,axis=1,keepdims=True))

def soft_cols(s):
    e=jnp.exp(s-jnp.max(s,axis=0,keepdims=True))
    return e*(1.0/jnp.sum(e,axis=0,keepdims=True))

def head(ref,h):
    return ref[h*HD:(h+1)*HD,:]

def marks_body(qkv_ref,marks_ref,k2_ref,peak_ref):
    heads=k2_ref.shape[0]
    length=qkv_ref.shape[2]
    seg=segments(length)
    factor=HD**-0.25
    scale=factor/(length//LANDMARKS)
    peak_ref[...]=jnp.zeros(peak_ref.shape,F32)
    for h in range(heads):
        rows=slice(h*HD,(h+1)*HD)
        found=[]
        for j in range(2):
            x=qkv_ref[j,rows,:]
            xh,xl=parts(x)
            m=(dot(seg,xh,1,1)+dot(seg,xl,1,1))*scale
            marks_ref[h,j]=m
            found.append(m)
        inner=dot3(found[0],found[1],1,1)
        k2=soft_rows(inner)
        k2_ref[h]=k2
        top=jnp.max(jnp.sum(k2,axis=0,keepdims=True),axis=1,keepdims=True)
        peak_ref[h:h+1,:]=jnp.broadcast_to(top,(1,128))

def band(taps_row):
    wide=jnp.broadcast_to(taps_row,(SPAN,taps_row.shape[1]))
    return pltpu.roll(wide,0,1,stride=1,stride_axis=0)

def windows(pad_ref,x,length):
    pad_ref[:,:REACH]=jnp.zeros((HD,REACH),BF)
    pad_ref[:,REACH+length:]=jnp.zeros((HD,REACH),BF)
    pad_ref[:,REACH:REACH+length]=low(x)
    return jnp.concatenate([pad_ref[:,b*SPAN:b*SPAN+SPAN+2*REACH] for b in range(length//SPAN)],axis=0)

def kernels_body(qkv_ref,marks_ref,taps_ref,k1_ref,k3_ref,sum_ref,conv_ref,pad_ref):
    length=qkv_ref.shape[2]
    factor=HD**-0.25
    ql=marks_ref[0,0]; kl=marks_ref[0,1]
    k1_ref[...]=soft_cols(dot3(kl,qkv_ref[0]*factor,1,0))
    k3=soft_rows(dot3(ql,qkv_ref[1]*factor,1,0))
    k3_ref[...]=k3
    v=qkv_ref[2]
    sum_ref[0]=dot(low(k3),low(v),1,1)
    wins=windows(pad_ref,v,length)
    out=dot(wins,low(band(taps_ref[0,0:1,:])),1,1)
    for b in range(length//SPAN):
        conv_ref[:,b*SPAN:(b+1)*SPAN]=out[b*HD:(b+1)*HD,:]

def eye():
    r=lax.broadcasted_iota(jnp.int32,(LANDMARKS,LANDMARKS),0)
    c=lax.broadcasted_iota(jnp.int32,(LANDMARKS,LANDMARKS),1)
    return jnp.where(r==c,1.0,0.0)

def mix_body(k2_ref,peak_ref,sum_ref,k1_ref,conv_ref,ctx_ref,hist_ref,fin_ref):
    heads=k2_ref.shape[0]
    ident=eye()
    k2=[k2_ref[h] for h in range(heads)]
    k2p=[parts(x) for x in k2]
    a=[k2[h].T*(1.0/peak_ref[h:h+1,0:1]) for h in range(heads)]
    for step in range(ITERS):
        ap=[parts(x) for x in a]
        p=[dot3(k2p[h],ap[h],1,0) for h in range(heads)]
        pp=[parts(x) for x in p]
        t=[15.0*ident-dot3(pp[h],7.0*ident-p[h],1,0) for h in range(heads)]
        u=[13.0*ident-dot3(pp[h],t[h],1,0) for h in range(heads)]
        for h in range(heads):
            hist_ref[h,step,0]=a[h]; hist_ref[h,step,1]=p[h]
            hist_ref[h,step,2]=t[h]; hist_ref[h,step,3]=u[h]
        a=[0.25*dot3(ap[h],u[h],1,0) for h in range(heads)]
    for h in range(heads):
        car=dot3(a[h],sum_ref[h],1,0)
        fin_ref[h,0]=a[h]; fin_ref[h,1]=car
        rows=slice(h*HD,(h+1)*HD)
        ctx_ref[rows,:]=(dot(low(car),low(k1_ref[rows,:]),0,0)+conv_ref[rows,:]).astype(BF)

def back_marks_body(g_ref,k1_ref,k2_ref,peak_ref,sum_ref,hist_ref,fin_ref,vwin_ref,dsum_ref,dk2_ref,dinv_ref,dtap_ref,pad_ref,gst_ref):
    heads=k2_ref.shape[0]
    length=g_ref.shape[1]
    ident=eye()
    dinv_ref[...]=jnp.zeros(dinv_ref.shape,F32)
    dtap_ref[...]=jnp.zeros(dtap_ref.shape,F32)
    k2p=[parts(k2_ref[h]) for h in range(heads)]
    da=[]
    for h in range(heads):
        rows=slice(h*HD,(h+1)*HD)
        dcar=dot(low(k1_ref[rows,:]),g_ref[rows,:],1,1)
        dp_=parts(dcar)
        da.append(dot3(dp_,sum_ref[h],1,1))
        dsum_ref[h]=dot3(fin_ref[h,0],dp_,0,0)
    dk2=[None]*heads
    for step in reversed(range(ITERS)):
        nxt=[]
        for h in range(heads):
            A=parts(hist_ref[h,step,0]); P=hist_ref[h,step,1]; T2=hist_ref[h,step,2]; T3=hist_ref[h,step,3]
            Pp=parts(P); D=parts(da[h])
            dT3=0.25*dot3(A,D,0,0)
            dAn=0.25*dot3(D,T3,1,1)
            d3=parts(dT3)
            dT2=-dot3(Pp,d3,0,0)
            d2=parts(dT2)
            dP=-dot3(d3,T2,1,1)-dot3(d2,7.0*ident-P,1,1)+dot3(Pp,d2,0,0)
            dPp=parts(dP)
            add=dot3(dPp,A,1,1)
            dk2[h]=add if dk2[h] is None else dk2[h]+add
            nxt.append(dAn+dot3(k2p[h],dPp,0,0))
        da=nxt
    for h in range(heads):
        inv=1.0/peak_ref[h:h+1,0:1]
        dk2_ref[h]=dk2[h]+da[h].T*inv
        prod=da[h]*k2_ref[h].T
        tot=jnp.sum(jnp.sum(prod,axis=0,keepdims=True),axis=1,keepdims=True)
        dinv_ref[h:h+1,:]=jnp.broadcast_to(tot,(1,128))
    width=SPAN+2*REACH
    r=lax.broadcasted_iota(jnp.int32,(SPAN,SPAN),0)
    c=lax.broadcasted_iota(jnp.int32,(SPAN,SPAN),1)
    flip=jnp.where(r+c==SPAN-1,1.0,0.0).astype(BF)
    for h in range(heads):
        wins=windows(pad_ref,vwin_ref[0,h*HD:(h+1)*HD,:],length)
        for b in range(length//SPAN):
            gst_ref[b*HD:(b+1)*HD,:]=g_ref[h*HD:(h+1)*HD,b*SPAN:(b+1)*SPAN]
        m=dot(low(dot(gst_ref[...],flip,1,0)),wins,0,0)
        m=pltpu.roll(m,0,1,stride=1,stride_axis=0)
        s=jnp.sum(m,axis=0,keepdims=True)
        dtap_ref[h:h+1,:]=s

def back_body(qkv_ref,g_ref,marks_ref,k1_ref,k3_ref,sum_ref,fin_ref,dsum_ref,taps_ref,dqs_ref,dks_ref,dv_ref,dmarks_ref,pad_ref):
    length=qkv_ref.shape[2]
    factor=HD**-0.25
    g=g_ref[...]
    car=low(fin_ref[0,1]); dsum=dsum_ref[0]
    k1=k1_ref[...]
    dk1=dot(car,g,1,0)
    ds1=low(k1*(dk1-jnp.sum(k1*dk1,axis=0,keepdims=True)))
    dqs_ref[...]=dot(low(marks_ref[0,1]),ds1,0,0)
    dmarks_ref[0,1]=dot(ds1,low(qkv_ref[0]*factor),1,1)
    k3=k3_ref[...]
    v=qkv_ref[2]
    dl=low(dsum)
    delta=jnp.sum(dsum*sum_ref[0],axis=1,keepdims=True)
    ds3=low(k3*(dot(dl,low(v),1,0)-delta))
    dks_ref[...]=dot(low(marks_ref[0,0]),ds3,0,0)
    dmarks_ref[0,0]=dot(ds3,low(qkv_ref[1]*factor),1,1)
    wins=windows(pad_ref,g,length)
    out=dot(wins,low(band(taps_ref[0,1:2,:])),1,1)
    dv=dot(dl,low(k3),0,0)
    for b in range(length//SPAN):
        dv_ref[:,b*SPAN:(b+1)*SPAN]=(dv[:,b*SPAN:(b+1)*SPAN]+out[b*HD:(b+1)*HD,:]).astype(BF)

def close_body(k2_ref,dk2_ref,own_ref,marks_ref,dmarks_ref,dqs_ref,dks_ref,dv_ref,out_ref):
    heads=k2_ref.shape[0]
    length=dqs_ref.shape[1]
    factor=HD**-0.25
    seg=segments(length)
    scale=factor/(length//LANDMARKS)
    for h in range(heads):
        rows=slice(h*HD,(h+1)*HD)
        k2=k2_ref[h]
        sums=jnp.sum(k2,axis=0,keepdims=True)
        hit=jnp.where(sums==jnp.max(sums,axis=1,keepdims=True),1.0,0.0)
        hit=hit*(1.0/jnp.sum(hit,axis=1,keepdims=True))
        dk2=dk2_ref[h]+hit*own_ref[h:h+1,0:1]
        ds2=k2*(dk2-jnp.sum(k2*dk2,axis=1,keepdims=True))
        dp=parts(ds2)
        dql=dmarks_ref[h,0]+dot3(dp,marks_ref[h,1],1,0)
        dkl=dmarks_ref[h,1]+dot3(dp,marks_ref[h,0],0,0)
        for j,(d,s_ref) in enumerate(((dql,dqs_ref),(dkl,dks_ref))):
            dh,dl=parts(d*scale)
            spread=dot(dh,seg,0,0)+dot(dl,seg,0,0)
            out_ref[j,rows,:]=(s_ref[rows,:]*factor+spread).astype(BF)
        out_ref[2,rows,:]=dv_ref[rows,:]

def tap_rows(conv):
    heads,count=conv.shape
    width=SPAN+2*REACH
    left=REACH-count//2
    pad=((0,0),(left,width-left-count))
    return jnp.stack([jnp.pad(conv,pad),jnp.pad(conv[:,::-1],pad)],axis=1)

VM=pl.BlockSpec(memory_space=pltpu.VMEM)
def sds(shape,dt=F32): return jax.ShapeDtypeStruct(shape,dt)
LIM=56*2**20
def params(): return pltpu.CompilerParams(vmem_limit_bytes=LIM)

def marks_call(qkv,heads):
    n=qkv.shape[2]
    return pl.pallas_call(marks_body,out_shape=(sds((heads,2,LANDMARKS,HD)),sds((heads,LANDMARKS,LANDMARKS)),sds((8,128))),
        in_specs=[pl.BlockSpec((2,heads*HD,n),lambda i:(0,0,0))],grid=(1,),
        out_specs=(pl.BlockSpec((heads,2,LANDMARKS,HD),lambda i:(0,0,0,0)),pl.BlockSpec((heads,LANDMARKS,LANDMARKS),lambda i:(0,0,0)),pl.BlockSpec((8,128),lambda i:(0,0))),
        name="marks",compiler_params=params())(qkv)

def kernels_call(qkv,marks,taps,heads):
    n=qkv.shape[2]
    row=lambda: pl.BlockSpec((HD,n),lambda h:(h,0))
    return pl.pallas_call(kernels_body,grid=(heads,),
        in_specs=[pl.BlockSpec((3,HD,n),lambda h:(0,h,0)),pl.BlockSpec((1,2,LANDMARKS,HD),lambda h:(h,0,0,0)),pl.BlockSpec((1,2,taps.shape[2]),lambda h:(h,0,0))],
        out_specs=(row(),row(),pl.BlockSpec((1,LANDMARKS,HD),lambda h:(h,0,0)),row()),
        out_shape=(sds((heads*HD,n)),sds((heads*HD,n)),sds((heads,LANDMARKS,HD)),sds((heads*HD,n))),
        scratch_shapes=[pltpu.VMEM((HD,n+2*REACH),BF)],name="kernels",compiler_params=params())(qkv,marks,taps)

def mix_call(k2,peak,summ,k1,conv,heads):
    n=k1.shape[1]
    return pl.pallas_call(mix_body,in_specs=[VM]*5,out_specs=(VM,VM,VM),
        out_shape=(sds((heads*HD,n),BF),sds((heads,ITERS,4,LANDMARKS,LANDMARKS)),sds((heads,2,LANDMARKS,LANDMARKS))),
        name="mix",compiler_params=params())(k2,peak,summ,k1,conv)

def back_marks_call(g,k1,k2,peak,summ,hist,fin,qkv,heads):
    n=g.shape[1]
    z=lambda r:(lambda i:(0,)*r)
    full=lambda s: pl.BlockSpec(s,z(len(s)))
    return pl.pallas_call(back_marks_body,grid=(1,),
        in_specs=[full(g.shape),full(k1.shape),full(k2.shape),full(peak.shape),full(summ.shape),full(hist.shape),full(fin.shape),pl.BlockSpec((1,heads*HD,n),lambda i:(2,0,0))],
        out_specs=(full((heads,LANDMARKS,HD)),full((heads,LANDMARKS,LANDMARKS)),full((8,128)),full((8,SPAN+2*REACH))),
        out_shape=(sds((heads,LANDMARKS,HD)),sds((heads,LANDMARKS,LANDMARKS)),sds((8,128)),sds((8,SPAN+2*REACH))),
        scratch_shapes=[pltpu.VMEM((HD,n+2*REACH),BF),pltpu.VMEM((n//SPAN*HD,SPAN),BF)],
        name="back_marks",compiler_params=params())(g,k1,k2,peak,summ,hist,fin,qkv)

def back_call(qkv,g,marks,k1,k3,summ,fin,dsum,taps,heads):
    n=g.shape[1]
    row=lambda: pl.BlockSpec((HD,n),lambda h:(h,0))
    sq=lambda: pl.BlockSpec((1,LANDMARKS,HD),lambda h:(h,0,0))
    two=lambda: pl.BlockSpec((1,2,LANDMARKS,HD),lambda h:(h,0,0,0))
    return pl.pallas_call(back_body,grid=(heads,),
        in_specs=[pl.BlockSpec((3,HD,n),lambda h:(0,h,0)),row(),two(),row(),row(),sq(),two(),sq(),pl.BlockSpec((1,2,taps.shape[2]),lambda h:(h,0,0))],
        out_specs=(row(),row(),row(),two()),
        out_shape=(sds((heads*HD,n)),sds((heads*HD,n)),sds((heads*HD,n),BF),sds((heads,2,LANDMARKS,HD))),
        scratch_shapes=[pltpu.VMEM((HD,n+2*REACH),BF)],name="back",compiler_params=params())(qkv,g,marks,k1,k3,summ,fin,dsum,taps)

def close_call(k2,dk2,own,marks,dmarks,dqs,dks,dv,heads):
    n=dqs.shape[1]
    return pl.pallas_call(close_body,in_specs=[VM]*8,out_specs=VM,out_shape=sds((3,heads*HD,n),BF),
        name="close",compiler_params=params())(k2,dk2,own,marks,dmarks,dqs,dks,dv)


def xor_pairs(size, bit):
    return [(i, i ^ bit) for i in range(size)]


def xor_swap(value, axis, bit):
    return lax.ppermute(value, axis, xor_pairs(lax.axis_size(axis), bit))


def power_of_two(size):
    return size & (size - 1) == 0


def everywhere(value, axis, combine, plain):
    size = lax.axis_size(axis)
    if not power_of_two(size):
        return plain(value, axis)
    bit = 1
    while bit < size:
        value = combine(value, xor_swap(value, axis, bit))
        bit *= 2
    return value


def sum_everywhere(value, axis):
    return everywhere(value, axis, jnp.add, lax.psum)


def gather_near(value):
    far = xor_swap(value, "tensor", 2)
    near = xor_swap(value, "tensor", 1)
    last = xor_swap(far, "tensor", 1)
    return jnp.concatenate([value, near, far, last], axis=0)


def scatter_near(value):
    rows = value.shape[0] // 4
    block = lambda j: value[j * rows : (j + 1) * rows]
    far = xor_swap(jnp.concatenate([block(3)], axis=0), "tensor", 1)
    near = xor_swap(block(1), "tensor", 1)
    sent = block(2).astype(F32) + far.astype(F32)
    got = xor_swap(sent.astype(BF), "tensor", 2)
    return block(0).astype(F32) + near.astype(F32) + got.astype(F32)


def reorder(value, axis):
    place = lax.axis_index("tensor")
    rows = value.shape[axis] // 4
    return jnp.concatenate(
        [lax.dynamic_slice_in_dim(value, (place ^ j) * rows, rows, axis) for j in range(4)], axis=axis
    )


def sum_at_owner(value, rows):
    count = lax.axis_size("fsdp")
    tiles = value.reshape(count, rows, *value.shape[1:])
    arrived = lax.all_to_all(tiles, "fsdp", split_axis=0, concat_axis=0, tiled=True)
    return arrived.astype(F32).sum(axis=0)


def gelu_tanh(value):
    return jax.nn.gelu(value, approximate=True)


def norm_forward(rows, gain, shift):
    center = rows - jnp.mean(rows, axis=-1, keepdims=True)
    spread = jnp.mean(center * center, axis=-1, keepdims=True)
    factor = lax.rsqrt(spread + 1e-05)
    normed = center * factor
    return (normed * gain + shift, normed, factor)


def norm_backward(cotan, normed, factor, gain):
    scaled = cotan * gain
    return factor * (
        scaled
        - jnp.mean(scaled, axis=-1, keepdims=True)
        - normed * jnp.mean(scaled * normed, axis=-1, keepdims=True)
    )


def norm_params(cotan, normed):
    return (jnp.sum(cotan * normed, axis=0), jnp.sum(cotan, axis=0))


def mul(spec, a, b, kind=F32):
    return jnp.einsum(spec, a, b, preferred_element_type=F32).astype(kind)


def shards(
    inputs,
    qkv_weight,
    out_weight,
    conv_weight,
    up_weight,
    down_weight,
    mix_gain,
    mix_bias,
    feed_gain,
    feed_bias,
    out_grad,
):
    place = lax.axis_index("tensor")
    columns = qkv_weight.shape[2]
    heads = columns // HD
    units = up_weight.shape[1]
    share = qkv_weight.shape[1]
    gathered_in = reorder(gather_near(inputs.astype(BF)), 0)
    w_qkv = lax.all_gather(qkv_weight, "fsdp", axis=1, tiled=True)
    packed = jnp.concatenate([up_weight, down_weight.T, out_weight.T], axis=1)
    w_rest = lax.all_gather(packed, "fsdp", axis=0, tiled=True)
    w_up = w_rest[:, :units]
    w_down = w_rest[:, units : 2 * units]
    w_out = w_rest[:, 2 * units :]
    qkv = mul("nd,kdc->kcn", gathered_in, w_qkv)
    conv_local = lax.dynamic_slice_in_dim(conv_weight, place * heads, heads, 0)
    taps = tap_rows(conv_local)
    marks, k2, peak_local = marks_call(qkv, heads)
    peak = everywhere(peak_local, "fsdp", jnp.maximum, lax.pmax)
    k1, k3, summary, conv = kernels_call(qkv, marks, taps, heads)
    context, hist, fin = mix_call(k2, peak, summary, k1, conv, heads)
    context_own = reorder(context, 1)
    attended = scatter_near(mul("cn,dc->nd", context_own, w_out, BF))
    mixed_rows, normed_mix, factor_mix = norm_forward(inputs + attended, mix_gain, mix_bias)
    mixed_low = gather_near(mixed_rows.astype(BF))
    up_rows = mul("nd,df->nf", mixed_low, w_up)
    act, gelu_back = jax.vjp(gelu_tanh, up_rows)
    act_low = act.astype(BF)
    fed = scatter_near(mul("nf,df->nd", act_low, w_down, BF))
    output, normed_feed, factor_feed = norm_forward(mixed_rows + fed, feed_gain, feed_bias)
    grad_feed = norm_backward(out_grad, normed_feed, factor_feed, feed_gain)
    feed_gain_part, feed_bias_part = norm_params(out_grad, normed_feed)
    grad_down = gather_near(grad_feed.astype(BF))
    grad_act = mul("nd,df->nf", grad_down, w_down)
    grad_up = gelu_back(grad_act)[0].astype(BF)
    grad_mixed_rows = grad_feed + scatter_near(mul("nf,df->nd", grad_up, w_up, BF))
    down_share = sum_at_owner(mul("nd,nf->df", grad_down, act_low, BF), share).T
    up_share = sum_at_owner(mul("nd,nf->df", mixed_low, grad_up, BF), share)
    grad_mix = norm_backward(grad_mixed_rows, normed_mix, factor_mix, mix_gain)
    mix_gain_part, mix_bias_part = norm_params(grad_mixed_rows, normed_mix)
    grad_attended = gather_near(grad_mix.astype(BF))
    out_share = sum_at_owner(mul("nd,cn->dc", grad_attended, context_own, BF), share).T
    grad_context = reorder(mul("nd,dc->cn", grad_attended, w_out, BF), 1)
    dsum, dk2, dinv, dtap = back_marks_call(grad_context, k1, k2, peak, summary, hist, fin, qkv, heads)
    first = SPAN - 1 + REACH - conv_weight.shape[1] // 2
    dtap = dtap[:, first : first + 128]
    norm_stack = jnp.stack([mix_gain_part, mix_bias_part, feed_gain_part, feed_bias_part])
    norm_rows = norm_stack.reshape(-1, 128)
    total = sum_everywhere(jnp.concatenate([dinv, dtap, norm_rows], axis=0), "fsdp")
    own = jnp.where(peak_local == peak, -total[:8] / (peak * peak), 0.0)
    dqs, dks, dv, dmarks = back_call(qkv, grad_context, marks, k1, k3, summary, fin, dsum, taps, heads)
    grad_qkv = close_call(k2, dk2, own, marks, dmarks, dqs, dks, dv, heads)
    conv_full = lax.dynamic_update_slice_in_dim(
        jnp.zeros((conv_weight.shape[0], 128), F32), total[8 : 8 + heads], place * heads, 0
    )
    total = sum_everywhere(jnp.concatenate([conv_full, total[16:]], axis=0), "tensor")
    conv_grad = total[: conv_weight.shape[0], : conv_weight.shape[1]]
    norm_sum = total[conv_weight.shape[0] :].reshape(norm_stack.shape)
    input_grad = grad_mix + scatter_near(reorder(mul("kcn,kdc->nd", grad_qkv, w_qkv, BF), 0))
    qkv_grad = mul("nd,kcn->dkc", gathered_in, grad_qkv, BF)
    qkv_share = jnp.moveaxis(sum_at_owner(qkv_grad, share), 0, 1)
    return (
        output,
        input_grad,
        qkv_share,
        out_share,
        conv_grad,
        up_share,
        down_share,
        norm_sum[0],
        norm_sum[1],
        norm_sum[2],
        norm_sum[3],
    )


def solution(mesh):
    rows = P(("fsdp", "tensor"), None)
    cross = P("tensor", "fsdp")
    stacked = P(None, "fsdp", "tensor")
    return jax.shard_map(
        shards,
        mesh=mesh,
        in_specs=(rows, stacked, cross, P(), P("fsdp", "tensor"), cross, P(), P(), P(), P(), rows),
        out_specs=(rows, rows, stacked, cross, P(), P("fsdp", "tensor"), cross, P(), P(), P(), P()),
        check_vma=False,
    )
```

time: 744 us -> 440 us (0.59)
  waiting for transfers between devices: 287 us -> 164 us
  matrix products: 143 us -> 52.4 us
  blocking collectives: 133 us -> 48.3 us
  other arithmetic: 90.6 us -> 35.8 us
  Pallas kernels: 0 us -> 46.4 us
  starting transfers between devices: 18.5 us -> 40.5 us
  local copies, waits for them, and re-layouts: 45 us -> 30.3 us
    ppermute x0 -> x32, waiting for transfers between devices: none -> 154 us  [xor_swap(): return lax.ppermute(value, axis, xor_pairs(lax.axis_size(axis), bit))]
    reduce_scatter x4 -> x0, waiting for transfers between devices: 130 us -> none  [the longest x1 55.7 us: shards(): lax.psum_scatter(jnp.dot(context, w_out, preferred_element_type=jnp.float...]
    all_gather x6 -> x1, waiting for transfers between devices: 105 us -> 0.02 us  [shards(): w_rest = lax.all_gather(packed, 'fsdp', axis=0, tiled=True)]
    dot_general x104 -> x11, matrix products: 143 us -> 45.4 us  [mul(): return jnp.einsum(spec, a, b, preferred_element_type=F32).astype(kind)]
    pallas_call x0 -> x6, Pallas kernels: none -> 46.4 us  [the longest x1 14.9 us: back_marks_call(): pl.pallas_call(back_marks_body, grid=(1,), in_specs=[full(g.shape), full(...]
    all_to_all x4, waiting for transfers between devices: 51.7 us -> 9.93 us  [sum_at_owner(): lax.all_to_all(tiles, 'fsdp', split_axis=0, concat_axis=0, tiled=True)]
    psum x1 -> x0, blocking collectives: 40 us -> none  [shards(): lax.psum((peak_full, conv_full, norm_stack), ('fsdp', 'tensor'))]
    all_gather x2 -> x1, blocking collectives: 73.4 us -> 48.3 us  [shards(): w_qkv = lax.all_gather(qkv_weight, 'fsdp', axis=1, tiled=True)]
  transfers between devices with their start and end apart: 14 -> 37, of which waited for: 10 -> 19; matrix products, arithmetic and copies ran while one was open for 24% -> 17% of each run, Pallas kernels for 0% -> 11%
where the time goes in v1:
time: 440 us; the launch traced here: 433 us
  waiting for transfers between devices  164 us (37%)
  matrix products  52.4 us (12%)
  blocking collectives  48.3 us (11%)
  Pallas kernels  46.4 us (11%)
  starting transfers between devices  40.5 us (9%)
  other arithmetic  35.8 us (8%)
  local copies, waits for them, and re-layouts  30.3 us (7%)
  between operations  15.1 us (3%)
    ppermute x32, waiting for transfers between devices, xor_swap(): return lax.ppermute(value, axis, xor_pairs(lax.axis_size(axis), bit))  154 us
    all_gather x1, blocking collectives, shards(): w_qkv = lax.all_gather(qkv_weight, 'fsdp', axis=1, tiled=True)  48.3 us
    dot_general x11, matrix products, mul(): return jnp.einsum(spec, a, b, preferred_element_type=F32).astype(kind)  45.4 us
    ppermute x32, starting transfers between devices, xor_swap(): return lax.ppermute(value, axis, xor_pairs(lax.axis_size(axis), bit))  23.8 us
    all_to_all x4, starting transfers between devices, sum_at_owner(): lax.all_to_all(tiles, 'fsdp', split_axis=0, concat_axis=0, tiled=True)  16.6 us
    pallas_call x1, Pallas kernels, back_marks_call(): pl.pallas_call(back_marks_body, grid=(1,), in_specs=[full(g.shape), full(...  14.9 us
    unnamed x109, local copies, waits for them, and re-layouts  13.2 us
    all_to_all x4, waiting for transfers between devices, sum_at_owner(): lax.all_to_all(tiles, 'fsdp', split_axis=0, concat_axis=0, tiled=True)  9.93 us
  transfers between devices with their start and end apart: 37, of which 19 were waited for; matrix products, arithmetic and copies ran while one was open for 17% of the time, Pallas kernels for 11%

profile of v1, /device:TPU:0, one launch (start us, length us, event | category | flops | bytes accessed | tf_op | source)
XLA Modules:
  0.0 433.3 jit_solution(5240792354812348506)
XLA Ops:
  11.4 3.1 collective-permute-start.1
  14.5 17.6 %collective-permute-done.1 = bf16[512,768]{1,0:T(8,128)(2,1)} collective-permute-done((bf16[512,768]{1,0:T(8,128)(2,1)S(1)}, bf16[512,768]{1,0:T(8,128)(2,1)}, u32[]{:S(2)}, u32[]{:S(2)}) %collective-permute-start.1) | collective-permute-done | bytes 786464 | tf_op jit(solution)/shard_map/ppermute | solution.py:280
  32.3 48.3 %all_gather.6 = bf16[3,768,192]{2,0,1:T(4,128)(2,1)S(1)} all-gather(bf16[3,96,192]{2,0,1:T(4,128)(2,1)S(1)} %copy.34), channel_id=1, replica_groups=mesh['fsdp'=8,'tensor'=4] {'fsdp'}, dimensions={1}, use_global_device_ids=true | all-gather | bytes 995328 | tf_op jit(solution)/shard_map/all_gather | solution.py:382
  81.5 2.0 pad_maximum_fusion
  83.8 7.1 %fusion.21 = f32[2048,576]{0,1} fusion(bf16[768,576]{0,1:T(8,128)(2,1)S(1)} %bitcast.47, bf16[512,768]{1,0:T(8,128)(2,1)S(1)} %get-tuple-element.90, bf16[512,768]{1,0:T(8,128)(2,1)S(1)} %get-tuple-element.91, bf16[512,768]{1,0:T(8,128)(2,1)S(1)} %get-tuple-element.92, bf16[512,768]{1,0:T(8,128)(2,1)S(1)} %get-tuple-element.89), kind=kOutput, calls=%fused_computation.61 | convolution fusion | flops 1824522240 | bytes 8749056
  90.9 4.3 marks.1
  95.5 3.5 collective-permute-done.3
  100.0 3.3 collective-permute-done.4
  105.1 6.8 %kernels.1 = (f32[192,2048]{1,0:T(8,128)}, f32[192,2048]{1,0:T(8,128)}, f32[3,64,64]{2,1,0:T(8,128)}, f32[192,2048]{1,0:T(8,128)}) custom-call(f32[3,192,2048]{2,1,0:T(8,128)} %bitcast.41, f32[3,2,64,64]{3,2,1,0:T(8,128)} %get-tuple-element.31.marks_ref, f32[3,2,512]{2,1,0:T(2,128)} %pad_maximum_fusion.20.taps_ref), custom_call_target="tpu_custom_call" | custom-call | tf_op jit(solution)/shard_map/kernels/pallas_call | solution.py:235
  112.5 7.6 %mix.1 = (bf16[192,2048]{1,0:T(8,128)(2,1)}, f32[3,6,4,64,64]{4,3,2,1,0:T(8,128)}, f32[3,2,64,64]{3,2,1,0:T(8,128)}) custom-call(f32[3,64,64]{2,1,0:T(8,128)} %get-tuple-element.29.k2_ref, f32[8,128]{1,0:T(8,128)} %max.11.peak_ref, f32[3,64,64]{2,1,0:T(8,128)} %get-tuple-element.32.sum_ref, f32[192,2048]{1,0:T(8,128)} %get-tuple-element.33.k1_ref, ...), custom_call_target="tpu_custom_call" | custom-call | tf_op jit(solution)/shard_map/mix/pallas_call | solution.py:243
  130.8 17.9 %collective-permute-done.8 = bf16[512,768]{0,1:T(8,128)(2,1)} collective-permute-done((bf16[512,768]{0,1:T(8,128)(2,1)}, bf16[512,768]{0,1:T(8,128)(2,1)}, u32[]{:S(2)}, u32[]{:S(2)}) %collective-permute-start.8) | collective-permute-done | bytes 786464 | tf_op jit(solution)/shard_map/ppermute | solution.py:280
  148.7 2.0 fusion.40
  152.9 17.2 %collective-permute-done.10 = bf16[512,768]{0,1:T(8,128)(2,1)S(1)} collective-permute-done((bf16[512,768]{0,1:T(8,128)(2,1)S(1)}, bf16[512,768]{0,1:T(8,128)(2,1)S(1)}, u32[]{:S(2)}, u32[]{:S(2)}) %collective-permute-start.10) | collective-permute-done | bytes 786464 | tf_op jit(solution)/shard_map/ppermute | solution.py:280
  170.1 2.3 collective-permute-done.11
  173.3 2.7 fusion.19
  176.1 3.4 convolution_convert_fusion.1
  187.6 16.5 %collective-permute-done.14 = bf16[512,768]{0,1:T(8,128)(2,1)} collective-permute-done((bf16[512,768]{0,1:T(8,128)(2,1)}, bf16[512,768]{0,1:T(8,128)(2,1)}, u32[]{:S(2)}, u32[]{:S(2)}) %collective-permute-start.14) | collective-permute-done | bytes 786464 | tf_op jit(solution)/shard_map/ppermute | solution.py:280
  204.1 2.4 fusion.39
  209.4 17.2 %collective-permute-done.16 = bf16[512,768]{0,1:T(8,128)(2,1)S(1)} collective-permute-done((bf16[512,768]{0,1:T(8,128)(2,1)S(1)}, bf16[512,768]{0,1:T(8,128)(2,1)S(1)}, u32[]{:S(2)}, u32[]{:S(2)}) %collective-permute-start.16) | collective-permute-done | bytes 786464 | tf_op jit(solution)/shard_map/ppermute | solution.py:280
  226.6 2.3 collective-permute-done.17
  228.9 7.2 %fusion.6 = bf16[2048,768]{1,0:T(8,128)(2,1)S(1)} fusion(f32[2048,768]{1,0:T(8,128)S(1)} %copy-done.50, bf16[768,1728]{1,0:T(8,128)(2,1)S(1)} %copy-done.42, bf16[512,768]{0,1:T(8,128)(2,1)S(1)} %collective-permute-done.17, bf16[512,768]{0,1:T(8,128)(2,1)S(1)} %collective-permute-done.16, bf16[512,768]{0,1:T(8,128)(2,1)S(1)} %collective-permute-done.15, ...), kind=kOutput, calls=%fused_computation.8 | convolution fusion | flops 2459959296 | bytes 13762560 | tf_op jit(solution)/shard_map/nd,df->nf/dot_general | solution.py:360
  236.2 2.9 convolution_convert_fusion
  243.5 18.1 %collective-permute-done.20 = bf16[512,768]{0,1:T(8,128)(2,1)S(1)} collective-permute-done((bf16[512,768]{0,1:T(8,128)(2,1)S(1)}, bf16[512,768]{0,1:T(8,128)(2,1)S(1)}, u32[]{:S(2)}, u32[]{:S(2)}) %collective-permute-start.20) | collective-permute-done | bytes 786464 | tf_op jit(solution)/shard_map/ppermute | solution.py:280
  261.5 3.1 multiply_reduce_fusion.1
  268.7 3.7 convolution_convert_fusion.4
  272.5 4.4 %all-to-all-start.3 = ((bf16[8,96,768]{2,1,0:T(8,128)(2,1)}), bf16[8,96,768]{2,1,0:T(8,128)(2,1)}, u32[]{:S(2)}, u32[]{:S(2)}) async-start(bf16[8,96,768]{2,1,0:T(8,128)(2,1)} %bitcast.45), calls=%async_computation.3 | async-start | bytes 2359296 | tf_op jit(solution)/shard_map/all_to_all | solution.py:330
  277.1 9.1 %collective-permute-done.22 = bf16[512,768]{0,1:T(8,128)(2,1)} collective-permute-done((bf16[512,768]{0,1:T(8,128)(2,1)}, bf16[512,768]{0,1:T(8,128)(2,1)}, u32[]{:S(2)}, u32[]{:S(2)}) %collective-permute-start.22) | collective-permute-done | bytes 786464 | tf_op jit(solution)/shard_map/ppermute | solution.py:280
  286.3 6.5 %convolution_convert_fusion.5 = bf16[768,768]{1,0:T(8,128)(2,1)} fusion(bf16[2048,768]{1,0:T(8,128)(2,1)} %copy-done.48, bf16[512,768]{0,1:T(8,128)(2,1)} %copy-done.45, bf16[512,768]{0,1:T(8,128)(2,1)} %copy-done.43, bf16[512,768]{0,1:T(8,128)(2,1)} %copy-done.44, bf16[512,768]{0,1:T(8,128)(2,1)} %copy-done.14), kind=kOutput, calls=%fused_computation.44 | convolution fusion | flops 2429091840 | bytes 7471104 | tf_op jit(solution)/shard_map/nd,nf->df/dot_general | solution.py:360
  293.4 2.8 convolution_convert_fusion.3
  296.3 8.8 %all-to-all-done.3 = bf16[8,96,768]{2,1,0:T(8,128)(2,1)} async-done(((bf16[8,96,768]{2,1,0:T(8,128)(2,1)}), bf16[8,96,768]{2,1,0:T(8,128)(2,1)}, u32[]{:S(2)}, u32[]{:S(2)}) %all-to-all-start.3) | async-done | bytes 1179680 | tf_op jit(solution)/shard_map/all_to_all | solution.py:330
  305.0 3.7 all-to-all-start.2
  309.9 14.9 %back_marks.1 = (f32[3,64,64]{2,1,0:T(8,128)}, f32[3,64,64]{2,1,0:T(8,128)}, f32[8,128]{1,0:T(8,128)}, f32[8,512]{1,0:T(8,128)}) custom-call(bf16[192,2048]{1,0:T(8,128)(2,1)} %pad_maximum_fusion.6.g_ref, f32[192,2048]{1,0:T(8,128)} %get-tuple-element.33.k1_ref, f32[3,64,64]{2,1,0:T(8,128)} %get-tuple-element.29.k2_ref, f32[8,128]{1,0:T(8,128)} %max.11.peak_ref, ...), custom_call_target="tpu_custom_call" | custom-call | tf_op jit(solution)/shard_map/back_marks/pallas_call | solution.py:251
  332.7 5.2 %collective-permute-done.25 = f32[40,128]{1,0:T(8,128)S(1)} collective-permute-done((f32[40,128]{1,0:T(8,128)S(1)}, f32[40,128]{1,0:T(8,128)S(1)}, u32[]{:S(2)}, u32[]{:S(2)}) %collective-permute-start.25) | collective-permute-done | bytes 20512 | tf_op jit(solution)/shard_map/ppermute | solution.py:280
  337.8 2.6 collective-permute-start.26
  340.4 4.0 convolution_convert_fusion.6
  345.7 7.1 %back.1 = (f32[192,2048]{1,0:T(8,128)}, f32[192,2048]{1,0:T(8,128)}, bf16[192,2048]{1,0:T(8,128)(2,1)}, f32[3,2,64,64]{3,2,1,0:T(8,128)}) custom-call(f32[3,192,2048]{2,1,0:T(8,128)} %bitcast.43, bf16[192,2048]{1,0:T(8,128)(2,1)} %pad_maximum_fusion.6.g_ref, f32[3,2,64,64]{3,2,1,0:T(8,128)} %get-tuple-element.31.marks_ref, ...), custom_call_target="tpu_custom_call" | custom-call | tf_op jit(solution)/shard_map/back/pallas_call | solution.py:263
  353.5 5.7 %close.1 = bf16[3,192,2048]{2,1,0:T(8,128)(2,1)} custom-call(f32[3,64,64]{2,1,0:T(8,128)} %get-tuple-element.29.k2_ref, f32[3,64,64]{2,1,0:T(8,128)} %get-tuple-element.38.dk2_ref, f32[8,128]{1,0:T(8,128)} %fusion.25.own_ref, f32[3,2,64,64]{3,2,1,0:T(8,128)} %get-tuple-element.31.marks_ref, f32[3,2,64,64]{3,2,1,0:T(8,128)} %get-tuple-element.43.dmarks_ref, ...), custom_call_target="tpu_custom_call" | custom-call | tf_op jit(solution)/shard_map/close/pallas_call | solution.py:271
  359.2 4.6 %bitcast_convert_fusion = bf16[2048,768]{0,1:T(8,128)(2,1)S(1)} fusion(bf16[3,768,192]{1,2,0:T(8,128)(2,1)S(1)} %copy-done.13, bf16[3,192,2048]{2,1,0:T(8,128)(2,1)} %close.1), kind=kOutput, calls=%fused_computation.9 | convolution fusion | flops 1813512192 | bytes 6389760 | tf_op jit(solution)/shard_map/kcn,kdc->nd/dot_general | solution.py:360
  365.9 3.7 all-to-all-start.1
  369.6 5.5 %fusion.9 = bf16[768,3,192]{0,2,1:T(8,128)(2,1)} fusion(bf16[3,192,2048]{2,1,0:T(8,128)(2,1)} %close.1, bf16[512,768]{1,0:T(8,128)(2,1)} %copy-done.16, bf16[512,768]{1,0:T(8,128)(2,1)} %copy-done.17, bf16[512,768]{1,0:T(8,128)(2,1)} %copy-done.18, bf16[512,768]{1,0:T(8,128)(2,1)} %copy-done.15), kind=kOutput, calls=%fused_computation.47 | convolution fusion | flops 1824964608 | bytes 6389760 | tf_op jit(solution)/shard_map/nd,kcn->dkc/dot_general | solution.py:360
  375.2 3.2 reshape.91
  378.3 2.7 copy.45
  382.1 4.8 %all-to-all-start = ((bf16[8,96,3,192]{1,3,2,0:T(8,128)(2,1)}), bf16[8,96,3,192]{1,3,2,0:T(8,128)(2,1)}, u32[]{:S(2)}, u32[]{:S(2)}) async-start(bf16[8,96,3,192]{1,3,2,0:T(8,128)(2,1)} %copy.45), calls=%async_computation | async-start | bytes 2359296 | tf_op jit(solution)/shard_map/all_to_all | solution.py:330
  388.6 2.2 convert_reduce_fusion
  392.2 2.6 add_convert_fusion
  398.5 16.8 %collective-permute-done.31 = f32[36,128]{1,0:T(8,128)S(1)} collective-permute-done((f32[36,128]{1,0:T(8,128)S(1)}, f32[36,128]{1,0:T(8,128)S(1)}, u32[]{:S(2)}, u32[]{:S(2)}) %collective-permute-start.31) | collective-permute-done | bytes 18464 | tf_op jit(solution)/shard_map/ppermute | solution.py:280
  419.7 3.5 add_add_fusion
  423.2 3.0 copy.49
  (229 shorter events, 68.3 us)
Async XLA Ops:
  7.2 88.3 %copy-start = (f32[12,33]{1,0:T(8,128)S(1)}, f32[12,33]{1,0:T(8,128)}, u32[]{:S(2)}) copy-start(f32[12,33]{1,0:T(8,128)} %param.14) | copy-start | bytes 4756
  7.2 24.9 %copy-start.27 = (bf16[3,96,192]{2,1,0:T(8,128)(2,1)S(1)}, bf16[3,96,192]{2,1,0:T(8,128)(2,1)}, u32[]{:S(2)}) copy-start(bf16[3,96,192]{2,1,0:T(8,128)(2,1)} %param.12) | copy-start | bytes 331780
  7.2 114.2 %all-gather.2.cloned.1.call-start = ((), (), s32[]{:S(2)}) async-start(), calls=%async_computation.4 | async-start | bytes 3096576 | tf_op jit(solution)/shard_map/all_gather | solution.py:384
  11.4 20.7 %collective-permute-start.1 = (bf16[512,768]{1,0:T(8,128)(2,1)S(1)}, bf16[512,768]{1,0:T(8,128)(2,1)}, u32[]{:S(2)}, u32[]{:S(2)}) collective-permute-start(bf16[512,768]{1,0:T(8,128)(2,1)S(1)} %convert_element_type.132), channel_id=1, source_target_pairs={{0,2},{1,3},{2,0},{3,1},{4,6},{5,7},{6,4},{7,5},{8,10},{9,11},{10,... | collective-permute-start | bytes 2359304 | tf_op jit(solution)/shard_map/ppermute | solution.py:280
  14.5 67.0 %collective-permute-start = (bf16[512,768]{1,0:T(8,128)(2,1)S(1)}, bf16[512,768]{1,0:T(8,128)(2,1)}, u32[]{:S(2)}, u32[]{:S(2)}) collective-permute-start(bf16[512,768]{1,0:T(8,128)(2,1)S(1)} %convert_element_type.132), channel_id=1, source_target_pairs={{0,1},{1,0},{2,3},{3,2},{4,5},{5,4},{6,7},{7,6},{8,9},{9,8},{10,11... | collective-permute-start | bytes 2359304 | tf_op jit(solution)/shard_map/ppermute | solution.py:280
  32.1 49.4 %collective-permute-start.2 = (bf16[512,768]{1,0:T(8,128)(2,1)}, bf16[512,768]{1,0:T(8,128)(2,1)}, u32[]{:S(2)}, u32[]{:S(2)}) collective-permute-start(bf16[512,768]{1,0:T(8,128)(2,1)} %collective-permute-done.1), channel_id=1, source_target_pairs={{0,1},{1,0},{2,3},{3,2},{4,5},{5,4},{6,7},{7,6},{8,9},{9,8},{10,11... | collective-permute-start | bytes 2359304 | tf_op jit(solution)/shard_map/ppermute | solution.py:280
  95.2 3.8 collective-permute-start.3
  99.7 3.6 collective-permute-start.4
  103.3 8.5 %collective-permute-start.5 = (f32[8,128]{1,0:T(8,128)S(1)}, f32[8,128]{1,0:T(8,128)S(1)}, u32[]{:S(2)}, u32[]{:S(2)}) collective-permute-start(f32[8,128]{1,0:T(8,128)S(1)} %max.10), channel_id=1, source_target_pairs={{0,16},{4,20},{8,24},{12,28},{16,0},{20,4},{24,8},{28,12},{1,17},{... | collective-permute-start | bytes 12296 | tf_op jit(solution)/shard_map/ppermute | solution.py:280
  125.3 2.3 collective-permute-start.7
  125.3 5.5 %collective-permute-start.6 = (bf16[512,768]{0,1:T(8,128)(2,1)}, bf16[512,768]{0,1:T(8,128)(2,1)}, u32[]{:S(2)}, u32[]{:S(2)}) collective-permute-start(bf16[512,768]{0,1:T(8,128)(2,1)} %get-tuple-element.87), channel_id=1, source_target_pairs={{0,1},{1,0},{2,3},{3,2},{4,5},{5,4},{6,7},{7,6},{8,9},{9,8},{10,11... | collective-permute-start | bytes 2359304 | tf_op jit(solution)/shard_map/ppermute | solution.py:280
  128.8 19.9 %collective-permute-start.8 = (bf16[512,768]{0,1:T(8,128)(2,1)}, bf16[512,768]{0,1:T(8,128)(2,1)}, u32[]{:S(2)}, u32[]{:S(2)}) collective-permute-start(bf16[512,768]{0,1:T(8,128)(2,1)} %add_convert_fusion.3), channel_id=1, source_target_pairs={{0,2},{1,3},{2,0},{3,1},{4,6},{5,7},{6,4},{7,5},{8,10},{9,11},{10,... | collective-permute-start | bytes 2359304 | tf_op jit(solution)/shard_map/ppermute | solution.py:280
  150.7 22.6 %copy-start.41 = (bf16[768,1728]{1,0:T(8,128)(2,1)S(1)}, bf16[768,1728]{1,0:T(8,128)(2,1)}, u32[]{:S(2)}) copy-start(bf16[768,1728]{1,0:T(8,128)(2,1)} %all-gather.2.cloned.1.call-done) | copy-start | bytes 7962628
  151.0 113.7 %copy-start.33 = (f32[512]{0:T(512)}, f32[512]{0:T(512)S(1)}, u32[]{:S(2)}) copy-start(f32[512]{0:T(512)S(1)} %add_rsqrt_fusion.1) | copy-start | bytes 6148
  151.3 18.8 %collective-permute-start.10 = (bf16[512,768]{0,1:T(8,128)(2,1)S(1)}, bf16[512,768]{0,1:T(8,128)(2,1)S(1)}, u32[]{:S(2)}, u32[]{:S(2)}) collective-permute-start(bf16[512,768]{0,1:T(8,128)(2,1)S(1)} %fusion.12), channel_id=1, source_target_pairs={{0,2},{1,3},{2,0},{3,1},{4,6},{5,7},{6,4},{7,5},{8,10},{9,11},{10,... | collective-permute-start | bytes 2359304 | tf_op jit(solution)/shard_map/ppermute | solution.py:280
  152.9 17.2 %collective-permute-start.9 = (bf16[512,768]{0,1:T(8,128)(2,1)S(1)}, bf16[512,768]{0,1:T(8,128)(2,1)S(1)}, u32[]{:S(2)}, u32[]{:S(2)}) collective-permute-start(bf16[512,768]{0,1:T(8,128)(2,1)S(1)} %fusion.12), channel_id=1, source_target_pairs={{0,1},{1,0},{2,3},{3,2},{4,5},{5,4},{6,7},{7,6},{8,9},{9,8},{10,11... | collective-permute-start | bytes 2359304 | tf_op jit(solution)/shard_map/ppermute | solution.py:280
  170.1 2.3 collective-permute-start.11
  180.7 2.3 collective-permute-start.13
  180.8 6.8 %collective-permute-start.12 = (bf16[512,768]{0,1:T(8,128)(2,1)}, bf16[512,768]{0,1:T(8,128)(2,1)}, u32[]{:S(2)}, u32[]{:S(2)}) collective-permute-start(bf16[512,768]{0,1:T(8,128)(2,1)} %get-tuple-element.85), channel_id=1, source_target_pairs={{0,1},{1,0},{2,3},{3,2},{4,5},{5,4},{6,7},{7,6},{8,9},{9,8},{10,11... | collective-permute-start | bytes 2359304 | tf_op jit(solution)/shard_map/ppermute | solution.py:280
  184.2 19.9 %collective-permute-start.14 = (bf16[512,768]{0,1:T(8,128)(2,1)}, bf16[512,768]{0,1:T(8,128)(2,1)}, u32[]{:S(2)}, u32[]{:S(2)}) collective-permute-start(bf16[512,768]{0,1:T(8,128)(2,1)} %add_convert_fusion.2), channel_id=1, source_target_pairs={{0,2},{1,3},{2,0},{3,1},{4,6},{5,7},{6,4},{7,5},{8,10},{9,11},{10,... | collective-permute-start | bytes 2359304 | tf_op jit(solution)/shard_map/ppermute | solution.py:280
  204.1 24.8 %copy-start.50 = (f32[2048,768]{1,0:T(8,128)S(1)}, f32[2048,768]{1,0:T(8,128)}, u32[]{:S(2)}) copy-start(f32[2048,768]{1,0:T(8,128)} %copy-done.49) | copy-start | bytes 18874372
  207.8 18.8 %collective-permute-start.16 = (bf16[512,768]{0,1:T(8,128)(2,1)S(1)}, bf16[512,768]{0,1:T(8,128)(2,1)S(1)}, u32[]{:S(2)}, u32[]{:S(2)}) collective-permute-start(bf16[512,768]{0,1:T(8,128)(2,1)S(1)} %fusion.37), channel_id=1, source_target_pairs={{0,2},{1,3},{2,0},{3,1},{4,6},{5,7},{6,4},{7,5},{8,10},{9,11},{10,... | collective-permute-start | bytes 2359304 | tf_op jit(solution)/shard_map/ppermute | solution.py:280
  209.4 17.2 %collective-permute-start.15 = (bf16[512,768]{0,1:T(8,128)(2,1)S(1)}, bf16[512,768]{0,1:T(8,128)(2,1)S(1)}, u32[]{:S(2)}, u32[]{:S(2)}) collective-permute-start(bf16[512,768]{0,1:T(8,128)(2,1)S(1)} %fusion.37), channel_id=1, source_target_pairs={{0,1},{1,0},{2,3},{3,2},{4,5},{5,4},{6,7},{7,6},{8,9},{9,8},{10,11... | collective-permute-start | bytes 2359304 | tf_op jit(solution)/shard_map/ppermute | solution.py:280
  226.6 2.3 collective-permute-start.17
  239.2 2.4 collective-permute-start.19
  239.4 4.0 collective-permute-start.18
  241.9 19.6 %collective-permute-start.20 = (bf16[512,768]{0,1:T(8,128)(2,1)S(1)}, bf16[512,768]{0,1:T(8,128)(2,1)S(1)}, u32[]{:S(2)}, u32[]{:S(2)}) collective-permute-start(bf16[512,768]{0,1:T(8,128)(2,1)S(1)} %add_convert_fusion.1), channel_id=1, source_target_pairs={{0,2},{1,3},{2,0},{3,1},{4,6},{5,7},{6,4},{7,5},{8,10},{9,11},{10,... | collective-permute-start | bytes 2359304 | tf_op jit(solution)/shard_map/ppermute | solution.py:280
  267.2 19.0 %collective-permute-start.22 = (bf16[512,768]{0,1:T(8,128)(2,1)}, bf16[512,768]{0,1:T(8,128)(2,1)}, u32[]{:S(2)}, u32[]{:S(2)}) collective-permute-start(bf16[512,768]{0,1:T(8,128)(2,1)} %fusion.38), channel_id=1, source_target_pairs={{0,2},{1,3},{2,0},{3,1},{4,6},{5,7},{6,4},{7,5},{8,10},{9,11},{10,... | collective-permute-start | bytes 2359304 | tf_op jit(solution)/shard_map/ppermute | solution.py:280
  272.5 32.6 %all-to-all-start.3 = ((bf16[8,96,768]{2,1,0:T(8,128)(2,1)}), bf16[8,96,768]{2,1,0:T(8,128)(2,1)}, u32[]{:S(2)}, u32[]{:S(2)}) async-start(bf16[8,96,768]{2,1,0:T(8,128)(2,1)} %bitcast.45), calls=%async_computation.3 | async-start | bytes 2359296 | tf_op jit(solution)/shard_map/all_to_all | solution.py:330
  277.0 16.4 %collective-permute-start.21 = (bf16[512,768]{0,1:T(8,128)(2,1)}, bf16[512,768]{0,1:T(8,128)(2,1)S(1)}, u32[]{:S(2)}, u32[]{:S(2)}) collective-permute-start(bf16[512,768]{0,1:T(8,128)(2,1)} %fusion.38), channel_id=1, source_target_pairs={{0,1},{1,0},{2,3},{3,2},{4,5},{5,4},{6,7},{7,6},{8,9},{9,8},{10,11... | collective-permute-start | bytes 2359304 | tf_op jit(solution)/shard_map/ppermute | solution.py:280
  286.3 7.2 %collective-permute-start.23 = (bf16[512,768]{0,1:T(8,128)(2,1)}, bf16[512,768]{0,1:T(8,128)(2,1)}, u32[]{:S(2)}, u32[]{:S(2)}) collective-permute-start(bf16[512,768]{0,1:T(8,128)(2,1)} %collective-permute-done.22), channel_id=1, source_target_pairs={{0,1},{1,0},{2,3},{3,2},{4,5},{5,4},{6,7},{7,6},{8,9},{9,8},{10,11... | collective-permute-start | bytes 2359304 | tf_op jit(solution)/shard_map/ppermute | solution.py:280
  305.0 60.9 %all-to-all-start.2 = ((bf16[8,96,768]{2,1,0:T(8,128)(2,1)}), bf16[8,96,768]{2,1,0:T(8,128)(2,1)S(1)}, u32[]{:S(2)}, u32[]{:S(2)}) async-start(bf16[8,96,768]{2,1,0:T(8,128)(2,1)} %bitcast.44), calls=%async_computation.2 | async-start | bytes 2359296 | tf_op jit(solution)/shard_map/all_to_all | solution.py:330
  309.9 30.5 %copy-start.20 = (bf16[192,512]{1,0:T(8,128)(2,1)S(1)}, bf16[192,512]{1,0:T(8,128)(2,1)}, u32[]{:S(2)}) copy-start(bf16[192,512]{1,0:T(8,128)(2,1)} %copy-done.19) | copy-start | bytes 589828
  309.9 30.5 %copy-start.22 = (bf16[192,512]{1,0:T(8,128)(2,1)S(1)}, bf16[192,512]{1,0:T(8,128)(2,1)}, u32[]{:S(2)}) copy-start(bf16[192,512]{1,0:T(8,128)(2,1)} %copy-done.21) | copy-start | bytes 589828
  309.9 30.5 %copy-start.24 = (bf16[192,512]{1,0:T(8,128)(2,1)S(1)}, bf16[192,512]{1,0:T(8,128)(2,1)}, u32[]{:S(2)}) copy-start(bf16[192,512]{1,0:T(8,128)(2,1)} %copy-done.23) | copy-start | bytes 589828
  309.9 30.5 %copy-start.26 = (bf16[192,512]{1,0:T(8,128)(2,1)S(1)}, bf16[192,512]{1,0:T(8,128)(2,1)}, u32[]{:S(2)}) copy-start(bf16[192,512]{1,0:T(8,128)(2,1)} %copy-done.25) | copy-start | bytes 589828
  309.9 30.5 %copy-start.47 = (bf16[512,768]{0,1:T(8,128)(2,1)S(1)}, bf16[512,768]{0,1:T(8,128)(2,1)}, u32[]{:S(2)}) copy-start(bf16[512,768]{0,1:T(8,128)(2,1)} %copy-done.46) | copy-start | bytes 2359300
  326.2 4.0 collective-permute-start.24
  330.9 6.9 %collective-permute-start.25 = (f32[40,128]{1,0:T(8,128)S(1)}, f32[40,128]{1,0:T(8,128)S(1)}, u32[]{:S(2)}, u32[]{:S(2)}) collective-permute-start(f32[40,128]{1,0:T(8,128)S(1)} %fusion.36), channel_id=1, source_target_pairs={{0,8},{4,12},{8,0},{12,4},{16,24},{20,28},{24,16},{28,20},{1,9},{5... | collective-permute-start | bytes 61448 | tf_op jit(solution)/shard_map/ppermute | solution.py:280
  337.8 15.0 %collective-permute-start.26 = (f32[40,128]{1,0:T(8,128)S(1)}, f32[40,128]{1,0:T(8,128)S(1)}, u32[]{:S(2)}, u32[]{:S(2)}) collective-permute-start(f32[40,128]{1,0:T(8,128)S(1)} %add.160), channel_id=1, source_target_pairs={{0,16},{4,20},{8,24},{12,28},{16,0},{20,4},{24,8},{28,12},{1,17},{... | collective-permute-start | bytes 61448 | tf_op jit(solution)/shard_map/ppermute | solution.py:280
  365.9 26.3 %collective-permute-start.28 = (bf16[512,768]{0,1:T(8,128)(2,1)}, bf16[512,768]{0,1:T(8,128)(2,1)}, u32[]{:S(2)}, u32[]{:S(2)}) collective-permute-start(bf16[512,768]{0,1:T(8,128)(2,1)} %get-tuple-element.82), channel_id=1, source_target_pairs={{0,1},{1,0},{2,3},{3,2},{4,5},{5,4},{6,7},{7,6},{8,9},{9,8},{10,11... | collective-permute-start | bytes 2359304 | tf_op jit(solution)/shard_map/ppermute | solution.py:280
  365.9 16.2 %all-to-all-start.1 = ((bf16[8,96,192]{1,2,0:T(8,128)(2,1)}), bf16[8,96,192]{1,2,0:T(8,128)(2,1)S(1)}, u32[]{:S(2)}, u32[]{:S(2)}) async-start(bf16[8,96,192]{1,2,0:T(8,128)(2,1)} %copy.47), calls=%async_computation.1 | async-start | bytes 786432 | tf_op jit(solution)/shard_map/all_to_all | solution.py:330
  382.1 35.1 %all-to-all-start = ((bf16[8,96,3,192]{1,3,2,0:T(8,128)(2,1)}), bf16[8,96,3,192]{1,3,2,0:T(8,128)(2,1)}, u32[]{:S(2)}, u32[]{:S(2)}) async-start(bf16[8,96,3,192]{1,3,2,0:T(8,128)(2,1)} %copy.45), calls=%async_computation | async-start | bytes 2359296 | tf_op jit(solution)/shard_map/all_to_all | solution.py:330
  391.7 3.7 collective-permute-start.30
  392.2 27.4 %copy-start.3 = (f32[512,768]{0,1:T(8,128)S(1)}, f32[512,768]{0,1:T(8,128)}, u32[]{:S(2)}) copy-start(f32[512,768]{0,1:T(8,128)} %copy-done.2) | copy-start | bytes 4718596
  392.2 27.4 %collective-permute-start.27 = (bf16[512,768]{0,1:T(8,128)(2,1)}, bf16[512,768]{0,1:T(8,128)(2,1)}, u32[]{:S(2)}, u32[]{:S(2)}) collective-permute-start(bf16[512,768]{0,1:T(8,128)(2,1)} %get-tuple-element.81), channel_id=1, source_target_pairs={{0,1},{1,0},{2,3},{3,2},{4,5},{5,4},{6,7},{7,6},{8,9},{9,8},{10,11... | collective-permute-start | bytes 2359304 | tf_op jit(solution)/shard_map/ppermute | solution.py:280
  394.8 24.8 %collective-permute-start.29 = (bf16[512,768]{0,1:T(8,128)(2,1)}, bf16[512,768]{0,1:T(8,128)(2,1)}, u32[]{:S(2)}, u32[]{:S(2)}) collective-permute-start(bf16[512,768]{0,1:T(8,128)(2,1)} %add_convert_fusion), channel_id=1, source_target_pairs={{0,2},{1,3},{2,0},{3,1},{4,6},{5,7},{6,4},{7,5},{8,10},{9,11},{10,... | collective-permute-start | bytes 2359304 | tf_op jit(solution)/shard_map/ppermute | solution.py:280
  396.1 19.2 %collective-permute-start.31 = (f32[36,128]{1,0:T(8,128)S(1)}, f32[36,128]{1,0:T(8,128)S(1)}, u32[]{:S(2)}, u32[]{:S(2)}) collective-permute-start(f32[36,128]{1,0:T(8,128)S(1)} %fusion.35), channel_id=1, source_target_pairs={{0,2},{1,3},{2,0},{3,1},{4,6},{5,7},{6,4},{7,5},{8,10},{9,11},{10,... | collective-permute-start | bytes 55304 | tf_op jit(solution)/shard_map/ppermute | solution.py:280
  (41 other events, 284.8 us)
Sparse Core Ops, SparseCore 0:
  10.2 82.5 all-gather.1
